TPU v7x, 32 devices: a whole 2x2x4 slice. The times are simulated.
32 devices in a mesh: gx: 8 (over y, x, core), gy: 4 (over z).
Axes of the slice: x: 2, y: 2, z: 4, core: 2. Of those that a mesh axis runs over, the one named last changes fastest.
Arguments:
- tokens: bfloat16 [4096, 2048], P(('gx', 'gy')), may hold values from -6 to 6
- expert_ids: int32 [4096, 8], P(('gx', 'gy')), may hold values from 0 to 31, all different within a row; in each aligned block of 128 rows (0 to 127, 128 to 255, ...) at most 96 rows name the same one
- w_gate: bfloat16 [32, 2048, 768], P(('gx', 'gy')), may hold values from -0.125 to 0.125
- w_up: bfloat16 [32, 2048, 768], P(('gx', 'gy')), may hold values from -0.125 to 0.125
- down_error: float32 [32, 768, 2048], P(('gx', 'gy')), may hold values from -18 to 18
Outputs:
- gram_error: float32 [32, 768, 2048], P(('gx', 'gy'))
Inputs may be any that keep to these rules, and one draw needn't show every extreme that they name: `expert_ids`: among the rows of one device no expert is named more than 96 times, a bound that some block reaches; every expert is named by some row; the 8 ids of a row are distinct.
All inputs are finite; a program needn't handle non-finite values.
Results may differ from a plain program's by a relative error of at most 0.0036.
Values may be sent and summed in bfloat16 or wider, within the bound.
A program may use at most 128 MiB of HBM per device.

v0:
```python
import jax
import jax.numpy as jnp
from jax import lax
from jax.experimental import pallas as pl
from jax.experimental.pallas import tpu as pltpu
from jax.sharding import PartitionSpec as P

MESH = pl.DeviceIdType.MESH
LANES = 128


def fused_kernel(
    x_ref, wg_hbm, wu_hbm, out_ref,
    tok, wg, wu, hid, acc, cnt,
    recv, precv, s_x, s_y, s_dx, s_dy, s_dz, s_p, s_up, s_dn, l_sem,
):
    gx = lax.axis_index("gx")
    z = lax.axis_index("gy")
    rows = x_ref.shape[0]
    half = rows // 2
    width = wg.shape[0]
    core = gx % 2
    px = (gx // 2) % 2
    py = gx // 4
    expert = gx * 4 + z

    def plane_of(a, b):
        return b * 2 + a

    here = plane_of(px, py)
    planes = (here, plane_of(1 - px, py), plane_of(px, 1 - py), plane_of(1 - px, 1 - py))

    def dev(a, b, c):
        return b * 4 + a * 2 + c

    x_dev = (dev(1 - px, py, core), z)
    y_dev = (dev(px, 1 - py, core), z)
    p_dev = (dev(px, py, 1 - core), z)
    up_dev = (gx, z + 1)
    dn_dev = (gx, z - 1)

    mirror = z // 2
    inner = z + (3 - 2 * z) * mirror

    def level(k):
        base = k + inner * (1 - 2 * k) * (1 - k // 2)
        return base + (3 - 2 * base) * mirror

    def block(plane, lev, c):
        return tok.at[plane, lev, pl.ds(c * rows, rows), :]

    def copy(src, dst, ssem, rsem, to):
        return pltpu.make_async_remote_copy(
            src_ref=src, dst_ref=dst, send_sem=ssem, recv_sem=rsem,
            device_id=to, device_id_type=MESH,
        )

    def piece_copy(j, k, h, ssem, to, src=None):
        lev = level(k)
        spot = tok.at[planes[j], lev, pl.ds(core * rows + h * half, half), :]
        start = spot if src is None else src.at[pl.ds(h * half, half), :]
        return copy(start, spot, ssem, recv.at[planes[j], lev, h], to)

    def partner_copy(j, k, src=None):
        lev = level(k)
        spot = block(planes[j], lev, core)
        return copy(spot if src is None else src, spot, s_p.at[j, k], precv.at[planes[j], lev], p_dev)

    def wait_piece(j, k, h):
        piece_copy(j, k, h, s_x.at[k, h], p_dev).wait_recv()

    def wait_partner(j, k):
        lev = level(k)
        spot = block(planes[j], lev, 1 - core)
        copy(spot, spot, s_p.at[j, k], precv.at[planes[j], lev], p_dev).wait_recv()

    def unit(j, k):
        wait_partner(j, k)
        lev = level(k)
        view = tok.at[planes[j], lev]
        named = view[:, pl.ds(width, LANES)].astype(jnp.float32)
        hit = jnp.max((named == expert.astype(jnp.float32)).astype(jnp.float32), axis=1, keepdims=True)
        cnt[...] += jnp.broadcast_to(jnp.sum(hit, axis=0, keepdims=True), cnt.shape)
        rows_in = view[:, pl.ds(0, width)]
        for n in range(bands):
            cols = pl.ds(n * step, step)
            gate = jnp.dot(rows_in, wg[:, cols], preferred_element_type=jnp.float32)
            upward = jnp.dot(rows_in, wu[:, cols], preferred_element_type=jnp.float32)
            value = gate / (1.0 + jnp.exp(-gate)) * upward
            hid[pl.ds((j % 2) * 2 * rows, 2 * rows), cols] = jnp.where(hit > 0.5, value, 0.0).astype(jnp.bfloat16)

    bands = 3
    step = hid.shape[1] // bands

    def gram():
        for n in range(bands):
            rest = pl.ds(n * step, hid.shape[1] - n * step)
            acc[pl.ds(n * step, step), rest] += lax.dot_general(
                hid[:, pl.ds(n * step, step)], hid[:, rest], (((0,), (0,)), ((), ())),
                preferred_element_type=jnp.float32,
            )

    barrier = pltpu.get_barrier_semaphore()
    for to in (x_dev, y_dev, p_dev):
        pl.semaphore_signal(barrier, inc=1, device_id=to, device_id_type=MESH)

    @pl.when(z < 3)
    def _():
        pl.semaphore_signal(barrier, inc=1, device_id=up_dev, device_id_type=MESH)

    @pl.when(z > 0)
    def _():
        pl.semaphore_signal(barrier, inc=1, device_id=dn_dev, device_id_type=MESH)

    local = pltpu.make_async_copy(x_ref, block(here, z, core), l_sem.at[0])
    load_g = pltpu.make_async_copy(wg_hbm, wg, l_sem.at[1])
    load_u = pltpu.make_async_copy(wu_hbm, wu, l_sem.at[2])
    local.start()
    load_g.start()
    load_u.start()
    pl.semaphore_wait(barrier, 4 + inner)

    middle = inner == 1
    centre_dev = (gx, z + 1 - 2 * mirror)
    outer_dev = (gx, z - 1 + 2 * mirror)

    def sends_up(k):
        return jnp.logical_and(level(k) <= z, z < 3)

    def sends_down(k):
        return jnp.logical_and(level(k) >= z, z > 0)

    def along_z(k, h, act, src=None):
        @pl.when(sends_up(k))
        def _():
            act(piece_copy(0, k, h, s_up.at[k, h], up_dev, src))

        @pl.when(sends_down(k))
        def _():
            act(piece_copy(0, k, h, s_dn.at[k, h], dn_dev, src))

    def start(c):
        c.start()

    def sent(c):
        c.wait_send()

    def across(k, act, src=None):
        for h in range(2):
            act(piece_copy(0, k, h, s_y.at[k, h], y_dev, src))
            act(piece_copy(0, k, 1 - h, s_x.at[k, 1 - h], x_dev, src))

    def diag_x(k):
        return piece_copy(2, k, 0, s_dx.at[k], x_dev)

    def diag_y(k):
        return piece_copy(1, k, 1, s_dy.at[k], y_dev)

    def diag_z(k, h, to):
        return piece_copy(3, k, h, s_dz.at[k, h], to)

    def take_column(k):
        for h in range(2):
            wait_piece(0, k, h)

    def relay_column(k):
        for h in range(2):
            wait_piece(0, k, h)
            along_z(k, h, start)

    def relay_diag(k, to):
        for h in range(2):
            wait_piece(3, k, h)
            diag_z(k, h, to).start()

    for h in range(2):
        along_z(0, h, start, x_ref)
    across(0, start, x_ref)
    partner_copy(0, 0, x_ref).start()
    acc[...] = jnp.zeros_like(acc)
    cnt[...] = jnp.zeros_like(cnt)
    local.wait()
    load_g.wait()
    load_u.wait()

    def turn(k, carry):
        unit(0, k)

        @pl.when(k < 2)
        def _():
            wait_piece(2, k, 0)
            diag_x(k).start()
            wait_piece(1, k, 1)
            diag_y(k).start()

        @pl.when(jnp.logical_and(k < 3, jnp.logical_not(middle)))
        def _():
            take_column(k + 1)

        @pl.when(jnp.logical_and(k == 0, middle))
        def _():
            for h in range(2):
                for n in (1, 2):
                    wait_piece(0, n, h)
                    along_z(n, h, start)

        @pl.when(k < 3)
        def _():
            across(k + 1, start)
            partner_copy(0, k + 1).start()

        @pl.when(k >= 2)
        def _():
            wait_piece(2, k, 0)
            wait_piece(1, k, 1)

        wait_piece(2, k, 1)
        wait_piece(1, k, 0)
        partner_copy(1, k).start()
        partner_copy(2, k).start()
        unit(1, k)
        gram()

        @pl.when(jnp.logical_and(k < 2, middle))
        def _():
            relay_diag(k, centre_dev)

        @pl.when(jnp.logical_and(k == 1, middle))
        def _():
            relay_diag(2, outer_dev)

        @pl.when(jnp.logical_and(k == 2, middle))
        def _():
            relay_diag(3, outer_dev)

        @pl.when(middle)
        def _():
            partner_copy(3, k).start()

        unit(2, k)

        @pl.when(jnp.logical_not(middle))
        def _():
            wait_piece(3, k, 0)
            wait_piece(3, k, 1)
            partner_copy(3, k).start()

        unit(3, k)
        gram()

        @pl.when(jnp.logical_and(k == 0, middle))
        def _():
            relay_column(3)

        return carry

    lax.fori_loop(0, 4, turn, 0)
    count = cnt[0:1, 0:1]
    for n in range(bands):
        for m in range(n, bands):
            part = acc[pl.ds(n * step, step), pl.ds(m * step, step)] / count
            out_ref[pl.ds(n * step, step), pl.ds(m * step, step)] = part
            if m > n:
                out_ref[pl.ds(m * step, step), pl.ds(n * step, step)] = part.T

    def drain(k, carry):
        for h in range(2):
            along_z(k, h, sent)
        across(k, sent)

        @pl.when(k < 2)
        def _():
            diag_x(k).wait_send()
            diag_y(k).wait_send()

        @pl.when(middle)
        def _():
            for h in range(2):
                diag_z(k, h, outer_dev).wait_send()

        for j in range(4):
            partner_copy(j, k).wait_send()
        return carry

    lax.fori_loop(0, 4, drain, 0)


def fused_local(tokens, expert_ids, w_gate, w_up, down_error):
    rows, width = tokens.shape
    hidden = w_gate.shape[2]
    named = jnp.pad(
        expert_ids.astype(jnp.bfloat16),
        ((0, 0), (0, LANES - expert_ids.shape[1])),
        constant_values=-1.0,
    )
    packed = jnp.concatenate([tokens, named], axis=1)
    vmem = pl.BlockSpec(memory_space=pltpu.VMEM)
    hbm = pl.BlockSpec(memory_space=pltpu.HBM)
    dma = pltpu.SemaphoreType.DMA
    mean_gram = pl.pallas_call(
        fused_kernel,
        out_shape=jax.ShapeDtypeStruct((hidden, hidden), jnp.float32),
        in_specs=[vmem, hbm, hbm],
        out_specs=vmem,
        scratch_shapes=[
            pltpu.VMEM((4, 4, 2 * rows, width + LANES), jnp.bfloat16),
            pltpu.VMEM((width, hidden), jnp.bfloat16),
            pltpu.VMEM((width, hidden), jnp.bfloat16),
            pltpu.VMEM((4 * rows, hidden), jnp.bfloat16),
            pltpu.VMEM((hidden, hidden), jnp.float32),
            pltpu.VMEM((8, LANES), jnp.float32),
            dma((4, 4, 2)), dma((4, 4)),
            dma((4, 2)), dma((4, 2)), dma((4,)), dma((4,)), dma((4, 2)),
            dma((4, 4)), dma((4, 2)), dma((4, 2)),
            dma((3,)),
        ],
        compiler_params=pltpu.CompilerParams(
            collective_id=0, has_side_effects=True, vmem_limit_bytes=56 * 1024 * 1024
        ),
    )(packed, w_gate[0], w_up[0])
    return jnp.dot(mean_gram, down_error[0], preferred_element_type=jnp.float32)[None]


def hidden_rows(received, w_gate, w_up):
    sources, slots, width = received.shape
    flat_rows = received.reshape(sources * slots, width)
    gate = jnp.dot(flat_rows, w_gate[0], preferred_element_type=jnp.float32)
    upward = jnp.dot(flat_rows, w_up[0], preferred_element_type=jnp.float32)
    hidden = (jax.nn.silu(gate) * upward).astype(jnp.bfloat16)
    return hidden.reshape(sources, slots, hidden.shape[1])


def cross_gram(first, second):
    return lax.dot_general(
        first, second, (((0,), (0,)), ((), ())), preferred_element_type=jnp.float32
    )


def gram_of(hidden):
    middle = hidden.shape[1] // 2
    left_part = hidden[:, :middle]
    right_part = hidden[:, middle:]
    upper_left = cross_gram(left_part, left_part)
    upper_right = cross_gram(left_part, right_part)
    lower_right = cross_gram(right_part, right_part)
    top_band = jnp.concatenate([upper_left, upper_right], axis=1)
    bottom_band = jnp.concatenate([upper_right.T, lower_right], axis=1)
    return jnp.concatenate([top_band, bottom_band], axis=0)


def local(tokens, expert_ids, w_gate, w_up, down_error):
    across = lax.axis_size("gx")
    within = lax.axis_size("gy")
    experts = across * within
    tok_count, top_count = expert_ids.shape
    width = tokens.shape[1]
    assigned = tok_count * top_count
    capacity = 3 * assigned // experts
    flat_ids = expert_ids.reshape(assigned)
    onehot = (flat_ids[:, None] == jnp.arange(experts, dtype=jnp.int32)[None, :]).astype(
        jnp.bfloat16
    )
    positions = jnp.arange(assigned, dtype=jnp.int32)
    lower = (positions[:, None] >= positions[None, :]).astype(jnp.bfloat16)
    running = jnp.dot(lower, onehot, preferred_element_type=jnp.float32)
    slot_of = (jnp.sum(running * onehot, axis=1) - 1.0).astype(jnp.int32)
    target = flat_ids * capacity + slot_of
    picked = tokens[positions // top_count]
    outgoing = jnp.zeros((experts * capacity, width), jnp.bfloat16).at[target].set(picked)
    tallies = jnp.sum(onehot.astype(jnp.float32), axis=0)
    loads = lax.psum_scatter(tallies, ("gx", "gy"), scatter_dimension=0, tiled=True)
    hidden = hidden_rows(
        lax.all_to_all(
            outgoing.reshape(experts, capacity, width),
            ("gx", "gy"),
            split_axis=0,
            concat_axis=0,
            tiled=True,
        ),
        w_gate,
        w_up,
    )
    hidden = hidden.reshape(experts * capacity, hidden.shape[2])
    gram = gram_of(hidden)
    mean_gram = gram / loads[0]
    product = jnp.dot(
        mean_gram,
        down_error[0],
        preferred_element_type=jnp.float32,
        precision=lax.Precision.HIGHEST,
    )
    return product[None]


def solution(mesh):
    small = mesh.shape["gx"] == 8 and mesh.shape["gy"] == 4
    return jax.shard_map(
        fused_local if small else local,
        mesh=mesh,
        in_specs=(
            P(("gx", "gy"), None),
            P(("gx", "gy"), None),
            P(("gx", "gy"), None, None),
            P(("gx", "gy"), None, None),
            P(("gx", "gy"), None, None),
        ),
        out_specs=P(("gx", "gy"), None, None),
        check_vma=False,
    )
```

profile of v0, /device:TPU:0, one launch (start us, length us, event | category | flops | bytes accessed | tf_op | source)
XLA Modules:
  0.0 88.3 jit_solution(11556262605469609757)
XLA Ops:
  0.0 0.7 convert_element_type.5
  0.7 0.1 copy.7
  0.8 1.9 %fusion.6.x_ref = bf16[128,2176]{1,0:T(8,128)(2,1)} fusion(bf16[128,8]{1,0:T(8,128)(2,1)S(1)} %copy.7, bf16[128,2048]{1,0:T(8,128)(2,1)} %param.5), kind=kLoop, calls=%fused_computation.5 | loop fusion | flops 1671168 | bytes 1083392 | tf_op jit(solution)/shard_map/concatenate | solution.py:296
  2.7 0.0 copy-start
  2.7 79.4 %shard_map.55 = f32[768,768]{1,0:T(8,128)} custom-call(bf16[128,2176]{1,0:T(8,128)(2,1)} %fusion.6.x_ref, bf16[2048,768]{1,0:T(8,128)(2,1)} %bitcast.19, bf16[2048,768]{1,0:T(8,128)(2,1)} %bitcast.20), custom_call_target="tpu_custom_call" | custom-call | tf_op jit(solution)/shard_map/pallas_call | solution.py:300
  82.2 0.0 copy-done
  82.2 6.1 %fusion.2 = f32[1,768,2048]{2,1,0:T(8,128)} fusion(f32[768,768]{1,0:T(8,128)} %shard_map.55, f32[1,768,2048]{2,1,0:T(8,128)S(1)} %copy-done), kind=kOutput, calls=%fused_computation.2 | convolution fusion | flops 2415919104 | bytes 14942208 | tf_op jit(solution)/shard_map/dot_general | solution.py:321
Async XLA Ops:
  2.7 79.5 %copy-start = (f32[1,768,2048]{2,1,0:T(8,128)S(1)}, f32[1,768,2048]{2,1,0:T(8,128)}, u32[]{:S(2)}) copy-start(f32[1,768,2048]{2,1,0:T(8,128)} %param.9) | copy-start | bytes 18874372
where the time goes:
time: 88.5 us; the launch traced here: 88.3 us
  Pallas kernels  79.4 us (90%)
  matrix products  6.13 us (7%)
  other arithmetic  2.58 us (3%)
    pallas_call x1, Pallas kernels, fused_local(): pl.pallas_call(fused_kernel, out_shape=jax.ShapeDtypeStruct((hidden, hidd...  79.4 us
    dot_general x1, matrix products, fused_local(): jnp.dot(mean_gram, down_error[0], preferred_element_type=jnp.float32)[None]  6.13 us
    concatenate x1, other arithmetic, fused_local(): packed = jnp.concatenate([tokens, named], axis=1)  1.89 us

commit v1 on v0

v1 whole, which is shorter than its diff:
```python
import jax
import jax.numpy as jnp
from jax import lax
from jax.experimental import pallas as pl
from jax.experimental.pallas import tpu as pltpu
from jax.sharding import PartitionSpec as P

MESH = pl.DeviceIdType.MESH
LANES = 128
VMEM_LIMIT = 59572224
FINISH_LIMIT = 16 * 1024 * 1024


STEPS = 10
CORNER, MIDDLE = 0, 1
FIRST = (0, 3, 5, 7)
FINISH_COLS = 256


def place(role, j, k, h):
    if j == 1:
        return FIRST[k] + 1 - h, 0
    if j == 2:
        return FIRST[k] + h, 1
    if j == 3 and k == 0:
        return 2, h
    if role == CORNER:
        if j == 3 and k == 3:
            return 9, h
        first = {(0, 1): 0, (0, 2): 2, (0, 3): 4, (3, 1): 6, (3, 2): 8}[j, k]
        return first + h, 2
    if j == 0 and k == 1:
        return (8, 2) if h == 0 else (9, 0)
    if j == 3 and k == 1:
        return 9, 1 + h
    first = {(0, 2): 0, (0, 3): 2, (3, 2): 4, (3, 3): 6}[j, k]
    return first + h, 2


def arrival(role, j, k, h):
    if role == MIDDLE and k == 1 and j in (0, 3):
        return h if j == 0 else 4 + h
    return place(role, j, k, h)[0]


def blocks():
    return [(j, k) for j in range(4) for k in range(4) if (j, k) != (0, 0)]


def arrivals(role, step):
    halves = [(j, k, h) for j, k in blocks() for h in range(2) if arrival(role, j, k, h) == step]
    ids = [(j, k) for j, k in blocks() if min(arrival(role, j, k, h) for h in range(2)) == step]
    return halves, ids


def sends(role, step):
    out = []

    def put(queue, block, halves, there, ids=True):
        if ids:
            out.append((queue, block, None, there))
        out.extend((queue, block, h, there) for h in halves)

    if step < 0:
        put("x", (0, 0), (1, 0), (1, 0))
        put("y", (0, 0), (0, 1), (2, 0))
        put("in", (0, 0), (0, 1), (0, 1) if role == CORNER else (0, 2))
        if role == MIDDLE:
            put("out", (0, 0), (0, 1), (0, 1))
    if step == 0:
        put("x", (2, 0), (0,), (3, 0))
        put("y", (1, 0), (1,), (3, 0), ids=False)
    columns = {1: (1,), 3: (2,), 5: (3,)} if role == CORNER else {1: (1, 2), 3: (3,)}
    for k in columns.get(step, ()):
        put("x", (0, k), (1, 0), (1, k))
        put("y", (0, k), (0, 1), (2, k))
    if role == CORNER:
        if step == 2:
            put("in", (3, 0), (0, 1), (3, 1))
        if step == 7:
            put("x", (2, 3), (0,), (3, 3))
            put("y", (1, 3), (1,), (3, 3), ids=False)
        return out
    if step in (0, 1):
        put("out", (0, 2), (step,), (0, 2), ids=step == 0)
        put("in", (0, 1), (step,), (0, 3), ids=step == 0)
    if step == 2:
        put("out", (0, 3), (0,), (0, 3))
        put("in", (3, 0), (0, 1), (3, 2))
    if step == 3:
        put("out", (0, 3), (1,), (0, 3), ids=False)
        put("out", (3, 0), (0, 1), (3, 1))
    if step in (4, 5):
        put("out", (3, 2), (step - 4,), (3, 2), ids=step == 4)
        put("in", (3, 1), (step - 4,), (3, 3), ids=step == 4)
    return out


def receiver(role, queue):
    if queue in ("x", "y"):
        return role
    return CORNER if queue == "out" else MIDDLE


def packed_tables():
    words = []
    for role in (CORNER, MIDDLE):
        held = {place(role, j, k, h): (j * 4 + k) * 2 + h for j, k in blocks() for h in range(2)}
        words.append([
            [sum(held[s, link] << (5 * (s % 6)) for s in range(first, min(first + 6, STEPS))) for first in (0, 6)]
            for link in range(3)
        ])
    return words


def gather_kernel(
    x_hbm, ids_hbm, wg_hbm, wu_hbm, out_ref,
    own, tok, idb, wg, wu, hid, acc, turned, mask,
    s_send, s_recv, s_idr, s_pair, s_part, s_load,
):
    gx = lax.axis_index("gx")
    z = lax.axis_index("gy")
    rows, width = x_hbm.shape
    half = rows // 2
    lot = 3 * rows
    core = gx % 2
    px = (gx // 2) % 2
    py = gx // 4
    expert = gx * 4 + z
    mirror = z // 2
    inner = z + (3 - 2 * z) * mirror

    def dev(a, b, c):
        return b * 4 + a * 2 + c

    inward = z + 1 - 2 * mirror
    target = {
        "x": (dev(1 - px, py, core), z),
        "y": (dev(px, 1 - py, core), z),
        "in": (gx, inward),
        "out": (gx, z - 1 + 2 * mirror),
        "pair": (dev(px, py, 1 - core), z),
    }

    def remote(src, dst, ssem, rsem, to):
        return pltpu.make_async_remote_copy(
            src_ref=src, dst_ref=dst, send_sem=ssem, recv_sem=rsem,
            device_id=target[to], device_id_type=MESH,
        )

    def spot(s, link, c):
        return tok.at[s, pl.ds((link * 2 + c) * half, half), :]

    def number(j, k):
        return j * 4 + k

    order = {}
    for role in (CORNER, MIDDLE):
        n = 0
        for step in range(-1, STEPS):
            for item in sends(role, step):
                order[role, item] = n
                n += 1

    def send_copy(role, item):
        queue, (j, k), h, there = item
        far = receiver(role, queue)
        ssem = s_send.at[order[role, item]]
        if h is None:
            src = ids_hbm if (j, k) == (0, 0) else idb.at[number(j, k), core]
            return remote(src, idb.at[number(*there), core], ssem, s_idr.at[number(*there)], queue)
        src = x_hbm.at[pl.ds(h * half, half), :] if (j, k) == (0, 0) else spot(*place(role, j, k, h), core)
        s, link = place(far, *there, h)
        return remote(src, spot(s, link, core), ssem, s_recv.at[s, link], queue)

    def pair_piece(s, link):
        return remote(spot(s, link, core), spot(s, link, core), s_pair.at[s * 3 + link], s_part.at[s * 3 + link], "pair")

    def pair_ids(b):
        n = 3 * STEPS + b
        src = ids_hbm if b == 0 else idb.at[b, core]
        return remote(src, idb.at[b, core], s_pair.at[n], s_part.at[n], "pair")

    n_own = 3 * STEPS + 16
    pair_own = remote(x_hbm, own.at[pl.ds(core * rows, rows), :], s_pair.at[n_own], s_part.at[n_own], "pair")

    def wait_piece(s, link):
        remote(spot(s, link, core), spot(s, link, core), s_send.at[0], s_recv.at[s, link], "pair").wait_recv()

    def wait_ids(b):
        remote(idb.at[b, core], idb.at[b, core], s_send.at[0], s_idr.at[b], "pair").wait_recv()

    def wait_pair_piece(s, link):
        n = s * 3 + link
        remote(spot(s, link, 1 - core), spot(s, link, 1 - core), s_send.at[0], s_part.at[n], "pair").wait_recv()

    def wait_pair_ids(b):
        n = 3 * STEPS + b
        remote(idb.at[b, 1 - core], idb.at[b, 1 - core], s_send.at[0], s_part.at[n], "pair").wait_recv()

    bands = 3
    features = hid.shape[1]
    band = features // bands

    def turn(b, c):
        hits = jnp.sum((idb[b, c] == expert).astype(jnp.float32), axis=0, keepdims=True)
        return jnp.broadcast_to(hits, (LANES, rows)).T

    def hidden(rows_in, count, base):
        live = jnp.concatenate([mask[pl.ds(0, count), :]] * (band // LANES), axis=1)
        for n in range(bands):
            cols = pl.ds(n * band, band)
            gate = jnp.dot(rows_in, wg[:, cols], preferred_element_type=jnp.float32)
            upward = jnp.dot(rows_in, wu[:, cols], preferred_element_type=jnp.float32)
            value = gate / (1.0 + jnp.exp(-gate)) * upward
            hid[pl.ds(base, count), cols] = jnp.where(live > 0.5, value, 0.0).astype(jnp.bfloat16)

    def gram(count, start):
        for n in range(bands):
            rest = pl.ds(n * band, features - n * band)
            part = lax.dot_general(
                hid[pl.ds(0, count), pl.ds(n * band, band)], hid[pl.ds(0, count), rest],
                (((0,), (0,)), ((), ())), preferred_element_type=jnp.float32,
            )
            if start:
                acc[pl.ds(n * band, band), rest] = part
            else:
                acc[pl.ds(n * band, band), rest] += part

    tables = packed_tables()

    def entry(link, s):
        corner, middle = tables[CORNER][link], tables[MIDDLE][link]
        low = corner[0] + (middle[0] - corner[0]) * inner
        high = corner[1] + (middle[1] - corner[1]) * inner
        word = low + (high - low) * (s // 6)
        return (word >> (5 * (s % 6))) % 32

    def unit(s):
        for link in range(3):
            held = entry(link, s)
            b, h = held // 2, held % 2
            for c in range(2):
                turned[link * 2 + c] = turn(b, c)
                mask[pl.ds((link * 2 + c) * half, half), :] = turned[link * 2 + c, pl.ds(pl.multiple_of(h * half, half), half), :]
        hidden(tok[s], lot, pl.multiple_of((s % 2) * lot, lot))

    barrier = pltpu.get_barrier_semaphore()
    for to in ("x", "y", "in", "pair"):
        pl.semaphore_signal(barrier, inc=1, device_id=target[to], device_id_type=MESH)

    @pl.when(inner == 1)
    def _():
        pl.semaphore_signal(barrier, inc=1, device_id=target["out"], device_id_type=MESH)

    local = pltpu.make_async_copy(x_hbm, own.at[pl.ds(core * rows, rows), :], s_load.at[0])
    local_ids = pltpu.make_async_copy(ids_hbm, idb.at[0, core], s_load.at[1])
    load_g = pltpu.make_async_copy(wg_hbm, wg, s_load.at[2])
    load_u = pltpu.make_async_copy(wu_hbm, wu, s_load.at[3])
    local.start()
    local_ids.start()
    load_g.start()
    load_u.start()
    pl.semaphore_wait(barrier, 4 + inner)

    roles = ((CORNER, inner == 0), (MIDDLE, inner == 1))
    for role, here in roles:
        @pl.when(here)
        def _():
            for item in sends(role, -1):
                send_copy(role, item).start()

    pair_ids(0).start()
    pair_own.start()
    local.wait()
    local_ids.wait()
    wait_pair_ids(0)
    theirs = own.at[pl.ds((1 - core) * rows, rows), :]
    remote(theirs, theirs, s_send.at[0], s_part.at[n_own], "pair").wait_recv()
    load_g.wait()
    load_u.wait()
    for c in range(2):
        mask[pl.ds(c * rows, rows), :] = turn(0, c)
    hidden(own[...], 2 * rows, 0)
    gram(2 * rows, True)

    def drain(role, step):
        for item in sends(role, step):
            send_copy(role, item).wait_send()
        if step < 0:
            pair_ids(0).wait_send()
            pair_own.wait_send()
            return
        halves, ids = arrivals(role, step)
        for j, k in ids:
            pair_ids(number(j, k)).wait_send()
        for j, k, h in halves:
            pair_piece(*place(role, j, k, h)).wait_send()

    late = 5

    def loop(s, carry):
        for role, here in roles:
            for step in range(STEPS + 1):
                @pl.when(jnp.logical_and(here, s == step))
                def _():
                    if step < STEPS:
                        halves, ids = arrivals(role, step)
                        for j, k in ids:
                            wait_ids(number(j, k))
                        for j, k, h in halves:
                            wait_piece(*place(role, j, k, h))
                        for item in sends(role, step):
                            send_copy(role, item).start()
                        for j, k in ids:
                            pair_ids(number(j, k)).start()
                        for j, k, h in halves:
                            pair_piece(*place(role, j, k, h)).start()
                    if step >= late - 1:
                        drain(role, step - late)
                    if step:
                        halves, ids = arrivals(role, step - 1)
                        for j, k in ids:
                            wait_pair_ids(number(j, k))
                        for j, k, h in halves:
                            wait_pair_piece(*place(role, j, k, h))

        @pl.when(s > 0)
        def _():
            unit(s - 1)

        @pl.when(jnp.logical_and(s > 0, s % 2 == 0))
        def _():
            gram(2 * lot, False)

        return carry

    lax.fori_loop(0, STEPS + 1, loop, 0)
    count = jnp.sum((idb[...] == expert).astype(jnp.float32))
    for n in range(bands):
        for m in range(n, bands):
            part = acc[pl.ds(n * band, band), pl.ds(m * band, band)] / count
            out_ref[pl.ds(n * band, band), pl.ds(m * band, band)] = part.astype(out_ref.dtype)
            if m > n:
                out_ref[pl.ds(m * band, band), pl.ds(n * band, band)] = part.T.astype(out_ref.dtype)
    for role, here in roles:
        @pl.when(here)
        def _():
            for step in range(STEPS + 1 - late, STEPS):
                drain(role, step)


def finish_kernel(gram_ref, error_ref, out_hbm, done, sem):
    cols = done.shape[2]
    turns = error_ref.shape[1] // cols

    def put(n):
        return pltpu.make_async_copy(done.at[n % 2], out_hbm.at[:, pl.ds(n * cols, cols)], sem.at[n % 2])

    for n in range(turns):
        if n >= 2:
            put(n - 2).wait()
        done[n % 2] = jnp.dot(
            gram_ref[...], error_ref[:, pl.ds(n * cols, cols)].astype(jnp.bfloat16),
            preferred_element_type=jnp.float32,
        )
        put(n).start()
    for n in range(turns - 2, turns):
        put(n).wait()


def fused_local(tokens, expert_ids, w_gate, w_up, down_error):
    rows, width = tokens.shape
    top = expert_ids.shape[1]
    features = w_gate.shape[2]
    vmem = pl.BlockSpec(memory_space=pltpu.VMEM)
    hbm = pl.BlockSpec(memory_space=pltpu.HBM)
    dma = pltpu.SemaphoreType.DMA
    n_sends = max(sum(len(sends(role, step)) for step in range(-1, STEPS)) for role in (CORNER, MIDDLE))
    pieces = 3 * STEPS + 17
    mean_gram = pl.pallas_call(
        gather_kernel,
        out_shape=jax.ShapeDtypeStruct((features, features), jnp.bfloat16),
        in_specs=[hbm] * 4,
        out_specs=vmem,
        scratch_shapes=[
            pltpu.VMEM((2 * rows, width), jnp.bfloat16),
            pltpu.VMEM((STEPS, 3 * rows, width), jnp.bfloat16),
            pltpu.VMEM((16, 2, top, rows), jnp.int32),
            pltpu.VMEM((width, features), jnp.bfloat16),
            pltpu.VMEM((width, features), jnp.bfloat16),
            pltpu.VMEM((6 * rows, features), jnp.bfloat16),
            pltpu.VMEM((features, features), jnp.float32),
            pltpu.VMEM((6, rows, LANES), jnp.float32),
            pltpu.VMEM((3 * rows, LANES), jnp.float32),
            dma((n_sends,)), dma((STEPS, 3)), dma((16,)), dma((pieces,)), dma((pieces,)), dma((4,)),
        ],
        compiler_params=pltpu.CompilerParams(
            collective_id=0, has_side_effects=True, vmem_limit_bytes=VMEM_LIMIT
        ),
    )(tokens, expert_ids.T, w_gate[0], w_up[0])
    return pl.pallas_call(
        finish_kernel,
        out_shape=jax.ShapeDtypeStruct(down_error.shape[1:], jnp.float32),
        in_specs=[vmem, vmem],
        out_specs=hbm,
        scratch_shapes=[pltpu.VMEM((2, features, FINISH_COLS), jnp.float32), dma((2,))],
        compiler_params=pltpu.CompilerParams(vmem_limit_bytes=FINISH_LIMIT),
    )(mean_gram, down_error[0])[None]


def hidden_rows(received, w_gate, w_up):
    sources, slots, width = received.shape
    flat_rows = received.reshape(sources * slots, width)
    gate = jnp.dot(flat_rows, w_gate[0], preferred_element_type=jnp.float32)
    upward = jnp.dot(flat_rows, w_up[0], preferred_element_type=jnp.float32)
    hidden = (jax.nn.silu(gate) * upward).astype(jnp.bfloat16)
    return hidden.reshape(sources, slots, hidden.shape[1])


def cross_gram(first, second):
    return lax.dot_general(
        first, second, (((0,), (0,)), ((), ())), preferred_element_type=jnp.float32
    )


def gram_of(hidden):
    middle = hidden.shape[1] // 2
    left_part = hidden[:, :middle]
    right_part = hidden[:, middle:]
    upper_left = cross_gram(left_part, left_part)
    upper_right = cross_gram(left_part, right_part)
    lower_right = cross_gram(right_part, right_part)
    top_band = jnp.concatenate([upper_left, upper_right], axis=1)
    bottom_band = jnp.concatenate([upper_right.T, lower_right], axis=1)
    return jnp.concatenate([top_band, bottom_band], axis=0)


def local(tokens, expert_ids, w_gate, w_up, down_error):
    across = lax.axis_size("gx")
    within = lax.axis_size("gy")
    experts = across * within
    tok_count, top_count = expert_ids.shape
    width = tokens.shape[1]
    assigned = tok_count * top_count
    capacity = 3 * assigned // experts
    flat_ids = expert_ids.reshape(assigned)
    onehot = (flat_ids[:, None] == jnp.arange(experts, dtype=jnp.int32)[None, :]).astype(
        jnp.bfloat16
    )
    positions = jnp.arange(assigned, dtype=jnp.int32)
    lower = (positions[:, None] >= positions[None, :]).astype(jnp.bfloat16)
    running = jnp.dot(lower, onehot, preferred_element_type=jnp.float32)
    slot_of = (jnp.sum(running * onehot, axis=1) - 1.0).astype(jnp.int32)
    target = flat_ids * capacity + slot_of
    picked = tokens[positions // top_count]
    outgoing = jnp.zeros((experts * capacity, width), jnp.bfloat16).at[target].set(picked)
    tallies = jnp.sum(onehot.astype(jnp.float32), axis=0)
    loads = lax.psum_scatter(tallies, ("gx", "gy"), scatter_dimension=0, tiled=True)
    hidden = hidden_rows(
        lax.all_to_all(
            outgoing.reshape(experts, capacity, width),
            ("gx", "gy"),
            split_axis=0,
            concat_axis=0,
            tiled=True,
        ),
        w_gate,
        w_up,
    )
    hidden = hidden.reshape(experts * capacity, hidden.shape[2])
    gram = gram_of(hidden)
    mean_gram = gram / loads[0]
    product = jnp.dot(
        mean_gram,
        down_error[0],
        preferred_element_type=jnp.float32,
        precision=lax.Precision.HIGHEST,
    )
    return product[None]


def solution(mesh):
    small = mesh.shape["gx"] == 8 and mesh.shape["gy"] == 4
    return jax.shard_map(
        fused_local if small else local,
        mesh=mesh,
        in_specs=(
            P(("gx", "gy"), None),
            P(("gx", "gy"), None),
            P(("gx", "gy"), None, None),
            P(("gx", "gy"), None, None),
            P(("gx", "gy"), None, None),
        ),
        out_specs=P(("gx", "gy"), None, None),
        check_vma=False,
    )
```

time: 88.5 us -> 80.9 us (0.914)
  matrix products: 6.13 us -> 0 us
  other arithmetic: 2.58 us -> 0 us
  local copies, waits for them, and re-layouts: 0.13 us -> 1.27 us
    dot_general x1 -> x0, matrix products: 6.13 us -> none  [fused_local(): jnp.dot(mean_gram, down_error[0], preferred_element_type=jnp.float32)[None]]
    concatenate x1 -> x0, other arithmetic: 1.89 us -> none  [fused_local(): packed = jnp.concatenate([tokens, named], axis=1)]
    unnamed x2 -> x4, local copies, waits for them, and re-layouts: 0.01 us -> 1.27 us
    pallas_call x1 -> x2, Pallas kernels: 79.4 us -> 79.5 us  [the longest x1 72.1 us: fused_local(): pl.pallas_call(gather_kernel, out_shape=jax.ShapeDtypeStruct((features, f...]
where the time goes in v1:
time: 80.9 us; the launch traced here: 80.8 us
  Pallas kernels  79.5 us (98%)
  local copies, waits for them, and re-layouts  1.27 us (2%)
    pallas_call x1, Pallas kernels, fused_local(): pl.pallas_call(gather_kernel, out_shape=jax.ShapeDtypeStruct((features, f...  72.1 us
    pallas_call x1, Pallas kernels, fused_local(): pl.pallas_call(finish_kernel, out_shape=jax.ShapeDtypeStruct(down_error.s...  7.33 us

profile of v1, /device:TPU:0, one launch (start us, length us, event | category | flops | bytes accessed | tf_op | source)
XLA Modules:
  0.0 80.8 jit_solution(10399799892945937094)
XLA Ops:
  0.0 0.0 copy-start
  0.0 72.1 %shard_map.55.gram_ref = bf16[768,768]{1,0:T(8,128)(2,1)} custom-call(bf16[128,2048]{1,0:T(8,128)(2,1)} %x_hbm.1, s32[8,128]{1,0:T(8,128)} %bitcast.8, bf16[2048,768]{1,0:T(8,128)(2,1)} %bitcast.6, bf16[2048,768]{1,0:T(8,128)(2,1)} %bitcast.7), custom_call_target="tpu_custom_call" | custom-call | tf_op jit(solution)/shard_map/pallas_call | solution.py:381
  72.1 0.0 copy-done
  72.2 0.0 copy-start.1
  72.2 1.3 %copy-done.1 = bf16[768,768]{1,0:T(8,128)(2,1)S(1)} copy-done((bf16[768,768]{1,0:T(8,128)(2,1)S(1)}, bf16[768,768]{1,0:T(8,128)(2,1)}, u32[]{:S(2)}) %copy-start.1) | copy-done | bytes 1179672
  73.4 7.3 %shard_map.56 = f32[768,2048]{1,0:T(8,128)} custom-call(bf16[768,768]{1,0:T(8,128)(2,1)S(1)} %copy-done.1, f32[768,2048]{1,0:T(8,128)S(1)} %bitcast.5), custom_call_target="tpu_custom_call" | custom-call | tf_op jit(solution)/shard_map/pallas_call | solution.py:402
Async XLA Ops:
  0.0 72.1 %copy-start = (f32[1,768,2048]{2,1,0:T(8,128)S(1)}, f32[1,768,2048]{2,1,0:T(8,128)}, u32[]{:S(2)}) copy-start(f32[1,768,2048]{2,1,0:T(8,128)} %param.9) | copy-start | bytes 18874372
  72.2 1.3 %copy-start.1 = (bf16[768,768]{1,0:T(8,128)(2,1)S(1)}, bf16[768,768]{1,0:T(8,128)(2,1)}, u32[]{:S(2)}) copy-start(bf16[768,768]{1,0:T(8,128)(2,1)} %shard_map.55.gram_ref) | copy-start | bytes 3538948

commit v2 on v1

--- a/solution.py
+++ b/solution.py
@@ -7,14 +7,14 @@
 
 MESH = pl.DeviceIdType.MESH
 LANES = 128
-VMEM_LIMIT = 59572224
+VMEM_LIMIT = 46000000
 FINISH_LIMIT = 16 * 1024 * 1024
 
 
 STEPS = 10
 CORNER, MIDDLE = 0, 1
 FIRST = (0, 3, 5, 7)
-FINISH_COLS = 256
+FINISH_COLS = 512
 
 
 def place(role, j, k, h):
@@ -48,9 +48,15 @@
 
 
 def arrivals(role, step):
-    halves = [(j, k, h) for j, k in blocks() for h in range(2) if arrival(role, j, k, h) == step]
+    filled = []
+    for j, k in blocks():
+        for h in range(2):
+            (s, link), come = place(role, j, k, h), arrival(role, j, k, h)
+            for q in (0, 1) if s == STEPS - 1 else (None,):
+                if step == (come + q if come == STEPS - 1 else come):
+                    filled.append((s, link, q))
     ids = [(j, k) for j, k in blocks() if min(arrival(role, j, k, h) for h in range(2)) == step]
-    return halves, ids
+    return filled, ids
 
 
 def sends(role, step):
@@ -114,14 +120,15 @@
 
 
 def gather_kernel(
-    x_hbm, ids_hbm, wg_hbm, wu_hbm, out_ref,
-    own, tok, idb, wg, wu, hid, acc, turned, mask,
+    x_hbm, ids_hbm, wg_hbm, wu_hbm, e_hbm, out_ref, error_ref,
+    own, tok, idb, wg, wu, hid, acc, error, turned, mask,
     s_send, s_recv, s_idr, s_pair, s_part, s_load,
 ):
     gx = lax.axis_index("gx")
     z = lax.axis_index("gy")
     rows, width = x_hbm.shape
     half = rows // 2
+    quarter = rows // 4
     lot = 3 * rows
     core = gx % 2
     px = (gx // 2) % 2
@@ -148,8 +155,15 @@
             device_id=target[to], device_id_type=MESH,
         )
 
-    def spot(s, link, c):
-        return tok.at[s, pl.ds((link * 2 + c) * half, half), :]
+    def spot(s, link, c, q=None):
+        if s < STEPS - 1:
+            first, count = ((link * 2 + c) * half, half) if q is None else ((link * 2 + c) * half + q * quarter, quarter)
+        else:
+            first, count = (q * 6 + link * 2 + c) * quarter, quarter
+        return tok.at[s, pl.ds(first, count), :]
+
+    def cuts(*steps):
+        return (0, 1) if max(steps) == STEPS - 1 else (None,)
 
     def number(j, k):
         return j * 4 + k
@@ -160,42 +174,55 @@
         for step in range(-1, STEPS):
             for item in sends(role, step):
                 order[role, item] = n
-                n += 1
-
-    def send_copy(role, item):
+                n += 2
+
+    def send_copies(role, item):
         queue, (j, k), h, there = item
         far = receiver(role, queue)
-        ssem = s_send.at[order[role, item]]
+        n = order[role, item]
         if h is None:
             src = ids_hbm if (j, k) == (0, 0) else idb.at[number(j, k), core]
-            return remote(src, idb.at[number(*there), core], ssem, s_idr.at[number(*there)], queue)
-        src = x_hbm.at[pl.ds(h * half, half), :] if (j, k) == (0, 0) else spot(*place(role, j, k, h), core)
+            return [remote(src, idb.at[number(*there), core], s_send.at[n], s_idr.at[number(*there)], queue)]
         s, link = place(far, *there, h)
-        return remote(src, spot(s, link, core), ssem, s_recv.at[s, link], queue)
-
-    def pair_piece(s, link):
-        return remote(spot(s, link, core), spot(s, link, core), s_pair.at[s * 3 + link], s_part.at[s * 3 + link], "pair")
+        mine = None if (j, k) == (0, 0) else place(role, j, k, h)
+        copies = []
+        for q in cuts(s, 0 if mine is None else mine[0]):
+            if mine is not None:
+                src = spot(*mine, core, q)
+            elif q is None:
+                src = x_hbm.at[pl.ds(h * half, half), :]
+            else:
+                src = x_hbm.at[pl.ds(h * half + q * quarter, quarter), :]
+            to = s + q if s == STEPS - 1 else s
+            copies.append(remote(src, spot(s, link, core, q), s_send.at[n + (q or 0)], s_recv.at[to, link], queue))
+        return copies
+
+    def pair_piece(s, link, q):
+        n = (s + (q or 0)) * 3 + link
+        return remote(spot(s, link, core, q), spot(s, link, core, q), s_pair.at[n], s_part.at[n], "pair")
 
     def pair_ids(b):
-        n = 3 * STEPS + b
+        n = 3 * STEPS + 3 + b
         src = ids_hbm if b == 0 else idb.at[b, core]
         return remote(src, idb.at[b, core], s_pair.at[n], s_part.at[n], "pair")
 
-    n_own = 3 * STEPS + 16
+    n_own = 3 * STEPS + 19
     pair_own = remote(x_hbm, own.at[pl.ds(core * rows, rows), :], s_pair.at[n_own], s_part.at[n_own], "pair")
 
-    def wait_piece(s, link):
-        remote(spot(s, link, core), spot(s, link, core), s_send.at[0], s_recv.at[s, link], "pair").wait_recv()
+    def wait_piece(s, link, q):
+        here = spot(s, link, core, q)
+        remote(here, here, s_send.at[0], s_recv.at[s + (q or 0), link], "pair").wait_recv()
 
     def wait_ids(b):
         remote(idb.at[b, core], idb.at[b, core], s_send.at[0], s_idr.at[b], "pair").wait_recv()
 
-    def wait_pair_piece(s, link):
-        n = s * 3 + link
-        remote(spot(s, link, 1 - core), spot(s, link, 1 - core), s_send.at[0], s_part.at[n], "pair").wait_recv()
+    def wait_pair_piece(s, link, q):
+        n = (s + (q or 0)) * 3 + link
+        there = spot(s, link, 1 - core, q)
+        remote(there, there, s_send.at[0], s_part.at[n], "pair").wait_recv()
 
     def wait_pair_ids(b):
-        n = 3 * STEPS + b
+        n = 3 * STEPS + 3 + b
         remote(idb.at[b, 1 - core], idb.at[b, 1 - core], s_send.at[0], s_part.at[n], "pair").wait_recv()
 
     bands = 3
@@ -215,11 +242,11 @@
             value = gate / (1.0 + jnp.exp(-gate)) * upward
             hid[pl.ds(base, count), cols] = jnp.where(live > 0.5, value, 0.0).astype(jnp.bfloat16)
 
-    def gram(count, start):
+    def gram(count, start, base=0):
         for n in range(bands):
             rest = pl.ds(n * band, features - n * band)
             part = lax.dot_general(
-                hid[pl.ds(0, count), pl.ds(n * band, band)], hid[pl.ds(0, count), rest],
+                hid[pl.ds(base, count), pl.ds(n * band, band)], hid[pl.ds(base, count), rest],
                 (((0,), (0,)), ((), ())), preferred_element_type=jnp.float32,
             )
             if start:
@@ -236,14 +263,14 @@
         word = low + (high - low) * (s // 6)
         return (word >> (5 * (s % 6))) % 32
 
-    def unit(s):
+    def marks(s, size, q=0):
         for link in range(3):
             held = entry(link, s)
             b, h = held // 2, held % 2
             for c in range(2):
                 turned[link * 2 + c] = turn(b, c)
-                mask[pl.ds((link * 2 + c) * half, half), :] = turned[link * 2 + c, pl.ds(pl.multiple_of(h * half, half), half), :]
-        hidden(tok[s], lot, pl.multiple_of((s % 2) * lot, lot))
+                first = pl.multiple_of(h * half + q * size, size)
+                mask[pl.ds((link * 2 + c) * size, size), :] = turned[link * 2 + c, pl.ds(first, size), :]
 
     barrier = pltpu.get_barrier_semaphore()
     for to in ("x", "y", "in", "pair"):
@@ -257,6 +284,7 @@
     local_ids = pltpu.make_async_copy(ids_hbm, idb.at[0, core], s_load.at[1])
     load_g = pltpu.make_async_copy(wg_hbm, wg, s_load.at[2])
     load_u = pltpu.make_async_copy(wu_hbm, wu, s_load.at[3])
+    load_e = pltpu.make_async_copy(e_hbm, error, s_load.at[4])
     local.start()
     local_ids.start()
     load_g.start()
@@ -268,7 +296,7 @@
         @pl.when(here)
         def _():
             for item in sends(role, -1):
-                send_copy(role, item).start()
+                [copy.start() for copy in send_copies(role, item)]
 
     pair_ids(0).start()
     pair_own.start()
@@ -279,6 +307,7 @@
     remote(theirs, theirs, s_send.at[0], s_part.at[n_own], "pair").wait_recv()
     load_g.wait()
     load_u.wait()
+    load_e.start()
     for c in range(2):
         mask[pl.ds(c * rows, rows), :] = turn(0, c)
     hidden(own[...], 2 * rows, 0)
@@ -286,56 +315,91 @@
 
     def drain(role, step):
         for item in sends(role, step):
-            send_copy(role, item).wait_send()
+            for copy in send_copies(role, item):
+                copy.wait_send()
         if step < 0:
             pair_ids(0).wait_send()
             pair_own.wait_send()
             return
-        halves, ids = arrivals(role, step)
+        filled, ids = arrivals(role, step)
         for j, k in ids:
             pair_ids(number(j, k)).wait_send()
-        for j, k, h in halves:
-            pair_piece(*place(role, j, k, h)).wait_send()
+        for slot in filled:
+            pair_piece(*slot).wait_send()
+
+    def take(role, step):
+        filled, ids = arrivals(role, step)
+        for j, k in ids:
+            wait_ids(number(j, k))
+        for slot in filled:
+            wait_piece(*slot)
+        for item in sends(role, step):
+            for copy in send_copies(role, item):
+                copy.start()
+        for j, k in ids:
+            pair_ids(number(j, k)).start()
+        for slot in filled:
+            pair_piece(*slot).start()
+
+    def join(role, step):
+        filled, ids = arrivals(role, step)
+        for j, k in ids:
+            wait_pair_ids(number(j, k))
+        for slot in filled:
+            wait_pair_piece(*slot)
 
     late = 5
 
-    def loop(s, carry):
+    def when_role(act, *args):
         for role, here in roles:
-            for step in range(STEPS + 1):
+            @pl.when(here)
+            def _():
+                act(role, *args)
+
+    def at_step(act, s, steps):
+        for role, here in roles:
+            for step in steps:
                 @pl.when(jnp.logical_and(here, s == step))
                 def _():
-                    if step < STEPS:
-                        halves, ids = arrivals(role, step)
-                        for j, k in ids:
-                            wait_ids(number(j, k))
-                        for j, k, h in halves:
-                            wait_piece(*place(role, j, k, h))
-                        for item in sends(role, step):
-                            send_copy(role, item).start()
-                        for j, k in ids:
-                            pair_ids(number(j, k)).start()
-                        for j, k, h in halves:
-                            pair_piece(*place(role, j, k, h)).start()
-                    if step >= late - 1:
-                        drain(role, step - late)
-                    if step:
-                        halves, ids = arrivals(role, step - 1)
-                        for j, k in ids:
-                            wait_pair_ids(number(j, k))
-                        for j, k, h in halves:
-                            wait_pair_piece(*place(role, j, k, h))
-
-        @pl.when(s > 0)
-        def _():
-            unit(s - 1)
+                    act(role, step)
+
+    full = range(STEPS - 1)
+
+    def loop(s, carry):
+        at_step(take, s, full)
+        at_step(lambda role, step: drain(role, step - late), s, full[late - 1:])
 
         @pl.when(jnp.logical_and(s > 0, s % 2 == 0))
         def _():
             gram(2 * lot, False)
 
+        @pl.when(s == 1)
+        def _():
+            load_e.wait()
+
+            def narrow(n, carry):
+                some = pl.ds(pl.multiple_of(n * LANES, LANES), LANES)
+                error_ref[some, :] = error[some, :].astype(jnp.bfloat16)
+                return carry
+
+            lax.fori_loop(0, features // LANES, narrow, 0)
+
+        at_step(join, s, full)
+        marks(s, half)
+        hidden(tok[s], lot, pl.multiple_of((s % 2) * lot, lot))
         return carry
 
-    lax.fori_loop(0, STEPS + 1, loop, 0)
+    lax.fori_loop(0, STEPS - 1, loop, 0)
+    last = STEPS - 1
+    part = 6 * quarter
+    for q in range(2):
+        when_role(take, last + q)
+        gram(part if q else lot, False, lot if q else 0)
+        when_role(drain, last + q - late)
+        when_role(join, last + q)
+        marks(last, quarter, q)
+        hidden(tok[last, pl.ds(q * part, part), :], part, lot if q == 0 else lot + part)
+    gram(part, False, lot + part)
     count = jnp.sum((idb[...] == expert).astype(jnp.float32))
     for n in range(bands):
         for m in range(n, bands):
@@ -346,26 +410,23 @@
     for role, here in roles:
         @pl.when(here)
         def _():
-            for step in range(STEPS + 1 - late, STEPS):
+            for step in range(STEPS + 1 - late, STEPS + 1):
                 drain(role, step)
 
 
 def finish_kernel(gram_ref, error_ref, out_hbm, done, sem):
-    cols = done.shape[2]
-    turns = error_ref.shape[1] // cols
+    turns, _, cols = done.shape
 
     def put(n):
-        return pltpu.make_async_copy(done.at[n % 2], out_hbm.at[:, pl.ds(n * cols, cols)], sem.at[n % 2])
+        return pltpu.make_async_copy(done.at[n], out_hbm.at[:, pl.ds(n * cols, cols)], sem.at[n])
 
     for n in range(turns):
-        if n >= 2:
-            put(n - 2).wait()
-        done[n % 2] = jnp.dot(
-            gram_ref[...], error_ref[:, pl.ds(n * cols, cols)].astype(jnp.bfloat16),
+        done[n] = jnp.dot(
+            gram_ref[...], error_ref[:, pl.ds(n * cols, cols)],
             preferred_element_type=jnp.float32,
         )
         put(n).start()
-    for n in range(turns - 2, turns):
+    for n in range(turns):
         put(n).wait()
 
 
@@ -376,13 +437,16 @@
     vmem = pl.BlockSpec(memory_space=pltpu.VMEM)
     hbm = pl.BlockSpec(memory_space=pltpu.HBM)
     dma = pltpu.SemaphoreType.DMA
-    n_sends = max(sum(len(sends(role, step)) for step in range(-1, STEPS)) for role in (CORNER, MIDDLE))
-    pieces = 3 * STEPS + 17
-    mean_gram = pl.pallas_call(
+    n_sends = 2 * max(sum(len(sends(role, step)) for step in range(-1, STEPS)) for role in (CORNER, MIDDLE))
+    pieces = 3 * STEPS + 20
+    mean_gram, narrow_error = pl.pallas_call(
         gather_kernel,
-        out_shape=jax.ShapeDtypeStruct((features, features), jnp.bfloat16),
-        in_specs=[hbm] * 4,
-        out_specs=vmem,
+        out_shape=(
+            jax.ShapeDtypeStruct((features, features), jnp.bfloat16),
+            jax.ShapeDtypeStruct((features, width), jnp.bfloat16),
+        ),
+        in_specs=[hbm] * 5,
+        out_specs=(vmem, vmem),
         scratch_shapes=[
             pltpu.VMEM((2 * rows, width), jnp.bfloat16),
             pltpu.VMEM((STEPS, 3 * rows, width), jnp.bfloat16),
@@ -391,22 +455,26 @@
             pltpu.VMEM((width, features), jnp.bfloat16),
             pltpu.VMEM((6 * rows, features), jnp.bfloat16),
             pltpu.VMEM((features, features), jnp.float32),
+            pltpu.VMEM((features, width), jnp.float32),
             pltpu.VMEM((6, rows, LANES), jnp.float32),
             pltpu.VMEM((3 * rows, LANES), jnp.float32),
-            dma((n_sends,)), dma((STEPS, 3)), dma((16,)), dma((pieces,)), dma((pieces,)), dma((4,)),
+            dma((n_sends,)), dma((STEPS + 1, 3)), dma((16,)), dma((pieces,)), dma((pieces,)), dma((5,)),
         ],
         compiler_params=pltpu.CompilerParams(
             collective_id=0, has_side_effects=True, vmem_limit_bytes=VMEM_LIMIT
         ),
-    )(tokens, expert_ids.T, w_gate[0], w_up[0])
+    )(*[
+        pltpu.with_memory_space_constraint(a, pltpu.HBM)
+        for a in (tokens, expert_ids.T, w_gate[0], w_up[0], down_error[0])
+    ])
     return pl.pallas_call(
         finish_kernel,
         out_shape=jax.ShapeDtypeStruct(down_error.shape[1:], jnp.float32),
         in_specs=[vmem, vmem],
         out_specs=hbm,
-        scratch_shapes=[pltpu.VMEM((2, features, FINISH_COLS), jnp.float32), dma((2,))],
+        scratch_shapes=[pltpu.VMEM((down_error.shape[2] // FINISH_COLS, features, FINISH_COLS), jnp.float32), dma((down_error.shape[2] // FINISH_COLS,))],
         compiler_params=pltpu.CompilerParams(vmem_limit_bytes=FINISH_LIMIT),
-    )(mean_gram, down_error[0])[None]
+    )(mean_gram, narrow_error)[None]
 
 
 def hidden_rows(received, w_gate, w_up):

time: 80.9 us -> 74.6 us (0.922)
  Pallas kernels: 79.5 us -> 73.9 us
  local copies, waits for them, and re-layouts: 1.27 us -> 0 us
    pallas_call x1, Pallas kernels: 7.33 us -> 3.78 us  [fused_local(): pl.pallas_call(finish_kernel, out_shape=jax.ShapeDtypeStruct(down_error.s...]
    pallas_call x1, Pallas kernels: 72.1 us -> 70.2 us  [fused_local(): pl.pallas_call(gather_kernel, out_shape=(jax.ShapeDtypeStruct((features,...]
    unnamed x4 -> x0, local copies, waits for them, and re-layouts: 1.27 us -> none
where the time goes in v2:
time: 74.6 us; the launch traced here: 73.9 us
  Pallas kernels  73.9 us (99%)
    pallas_call x1, Pallas kernels, fused_local(): pl.pallas_call(gather_kernel, out_shape=(jax.ShapeDtypeStruct((features,...  70.2 us
    pallas_call x1, Pallas kernels, fused_local(): pl.pallas_call(finish_kernel, out_shape=jax.ShapeDtypeStruct(down_error.s...  3.78 us

profile of v2, /device:TPU:0, one launch (start us, length us, event | category | flops | bytes accessed | tf_op | source)
XLA Modules:
  0.0 73.9 jit_solution(3571538061171143955)
XLA Ops:
  0.0 70.2 %shard_map.55 = (bf16[768,768]{1,0:T(8,128)(2,1)S(1)}, bf16[768,2048]{1,0:T(8,128)(2,1)S(1)}) custom-call(bf16[128,2048]{1,0:T(8,128)(2,1)} %x_hbm.1, s32[8,128]{1,0:T(8,128)} %bitcast.8, bf16[2048,768]{1,0:T(8,128)(2,1)} %bitcast.6, bf16[2048,768]{1,0:T(8,128)(2,1)} %bitcast.7, f32[768,2048]{1,0:T(8,128)} %bitcast.5), custom_call_target="tpu_custom_call" | custom-call | tf_op jit(solution)/shard_map/pallas_call | solution.py:442
  70.2 3.8 %shard_map.56 = f32[768,2048]{1,0:T(8,128)} custom-call(bf16[768,768]{1,0:T(8,128)(2,1)S(1)} %get-tuple-element.7.gram_ref, bf16[768,2048]{1,0:T(8,128)(2,1)S(1)} %get-tuple-element.8.error_ref), custom_call_target="tpu_custom_call" | custom-call | tf_op jit(solution)/shard_map/pallas_call | solution.py:470

commit v3 on v2

--- a/solution.py
+++ b/solution.py
@@ -47,6 +47,10 @@
     return [(j, k) for j in range(4) for k in range(4) if (j, k) != (0, 0)]
 
 
+def ids_arrival(role, j, k):
+    return max(0, min(arrival(role, j, k, h) for h in range(2)) - 1)
+
+
 def arrivals(role, step):
     filled = []
     for j, k in blocks():
@@ -55,7 +59,7 @@
             for q in (0, 1) if s == STEPS - 1 else (None,):
                 if step == (come + q if come == STEPS - 1 else come):
                     filled.append((s, link, q))
-    ids = [(j, k) for j, k in blocks() if min(arrival(role, j, k, h) for h in range(2)) == step]
+    ids = [(j, k) for j, k in blocks() if ids_arrival(role, j, k) == step]
     return filled, ids
 
 
@@ -157,9 +161,9 @@
 
     def spot(s, link, c, q=None):
         if s < STEPS - 1:
-            first, count = ((link * 2 + c) * half, half) if q is None else ((link * 2 + c) * half + q * quarter, quarter)
+            first, count = ((c * 3 + link) * half, half) if q is None else ((c * 3 + link) * half + q * quarter, quarter)
         else:
-            first, count = (q * 6 + link * 2 + c) * quarter, quarter
+            first, count = (q * 6 + c * 3 + link) * quarter, quarter
         return tok.at[s, pl.ds(first, count), :]
 
     def cuts(*steps):
@@ -181,7 +185,7 @@
         far = receiver(role, queue)
         n = order[role, item]
         if h is None:
-            src = ids_hbm if (j, k) == (0, 0) else idb.at[number(j, k), core]
+            src = idb.at[number(j, k), core]
             return [remote(src, idb.at[number(*there), core], s_send.at[n], s_idr.at[number(*there)], queue)]
         s, link = place(far, *there, h)
         mine = None if (j, k) == (0, 0) else place(role, j, k, h)
@@ -190,9 +194,9 @@
             if mine is not None:
                 src = spot(*mine, core, q)
             elif q is None:
-                src = x_hbm.at[pl.ds(h * half, half), :]
+                src = own.at[pl.ds(core * rows + h * half, half), :]
             else:
-                src = x_hbm.at[pl.ds(h * half + q * quarter, quarter), :]
+                src = own.at[pl.ds(core * rows + h * half + q * quarter, quarter), :]
             to = s + q if s == STEPS - 1 else s
             copies.append(remote(src, spot(s, link, core, q), s_send.at[n + (q or 0)], s_recv.at[to, link], queue))
         return copies
@@ -203,11 +207,11 @@
 
     def pair_ids(b):
         n = 3 * STEPS + 3 + b
-        src = ids_hbm if b == 0 else idb.at[b, core]
-        return remote(src, idb.at[b, core], s_pair.at[n], s_part.at[n], "pair")
+        return remote(idb.at[b, core], idb.at[b, core], s_pair.at[n], s_part.at[n], "pair")
 
     n_own = 3 * STEPS + 19
-    pair_own = remote(x_hbm, own.at[pl.ds(core * rows, rows), :], s_pair.at[n_own], s_part.at[n_own], "pair")
+    mine = own.at[pl.ds(core * rows, rows), :]
+    pair_own = remote(mine, mine, s_pair.at[n_own], s_part.at[n_own], "pair")
 
     def wait_piece(s, link, q):
         here = spot(s, link, core, q)
@@ -229,18 +233,26 @@
     features = hid.shape[1]
     band = features // bands
 
-    def turn(b, c):
-        hits = jnp.sum((idb[b, c] == expert).astype(jnp.float32), axis=0, keepdims=True)
-        return jnp.broadcast_to(hits, (LANES, rows)).T
-
-    def hidden(rows_in, count, base):
-        live = jnp.concatenate([mask[pl.ds(0, count), :]] * (band // LANES), axis=1)
+    def hits(b, c):
+        return jnp.sum((idb[b, c] == expert).astype(jnp.float32), axis=0, keepdims=True)
+
+    def turn(rows_of):
+        spare = jnp.zeros((8 - len(rows_of), rows), jnp.float32)
+        turned[...] = jnp.concatenate(rows_of + [spare], axis=0).T
+
+    def spread(group, first, count, to):
+        mask[pl.ds(to, count), :] = jnp.broadcast_to(turned[pl.ds(first, count), group:group + 1], (count, LANES))
+
+    def hidden(rows_in, count, base, first=0, between=None):
+        live = jnp.concatenate([mask[pl.ds(first, count), :]] * (band // LANES), axis=1)
         for n in range(bands):
             cols = pl.ds(n * band, band)
             gate = jnp.dot(rows_in, wg[:, cols], preferred_element_type=jnp.float32)
             upward = jnp.dot(rows_in, wu[:, cols], preferred_element_type=jnp.float32)
             value = gate / (1.0 + jnp.exp(-gate)) * upward
             hid[pl.ds(base, count), cols] = jnp.where(live > 0.5, value, 0.0).astype(jnp.bfloat16)
+            if between is not None and n == bands - 2:
+                between()
 
     def gram(count, start, base=0):
         for n in range(bands):
@@ -263,14 +275,13 @@
         word = low + (high - low) * (s // 6)
         return (word >> (5 * (s % 6))) % 32
 
-    def marks(s, size, q=0):
-        for link in range(3):
-            held = entry(link, s)
-            b, h = held // 2, held % 2
-            for c in range(2):
-                turned[link * 2 + c] = turn(b, c)
-                first = pl.multiple_of(h * half + q * size, size)
-                mask[pl.ds((link * 2 + c) * size, size), :] = turned[link * 2 + c, pl.ds(first, size), :]
+    def marks(s, size, parts=1, base=0):
+        held = [entry(link, s) for link in range(3)]
+        turn([hits(held[link] // 2, c) for c in range(2) for link in range(3)])
+        for q in range(parts):
+            for group in range(6):
+                first = pl.multiple_of(held[group % 3] % 2 * half + q * size, size)
+                spread(group, first, size, base + (q * 6 + group) * size)
 
     barrier = pltpu.get_barrier_semaphore()
     for to in ("x", "y", "in", "pair"):
@@ -280,7 +291,7 @@
     def _():
         pl.semaphore_signal(barrier, inc=1, device_id=target["out"], device_id_type=MESH)
 
-    local = pltpu.make_async_copy(x_hbm, own.at[pl.ds(core * rows, rows), :], s_load.at[0])
+    local = pltpu.make_async_copy(x_hbm, mine, s_load.at[0])
     local_ids = pltpu.make_async_copy(ids_hbm, idb.at[0, core], s_load.at[1])
     load_g = pltpu.make_async_copy(wg_hbm, wg, s_load.at[2])
     load_u = pltpu.make_async_copy(wu_hbm, wu, s_load.at[3])
@@ -289,6 +300,8 @@
     local_ids.start()
     load_g.start()
     load_u.start()
+    local.wait()
+    local_ids.wait()
     pl.semaphore_wait(barrier, 4 + inner)
 
     roles = ((CORNER, inner == 0), (MIDDLE, inner == 1))
@@ -300,16 +313,15 @@
 
     pair_ids(0).start()
     pair_own.start()
-    local.wait()
-    local_ids.wait()
     wait_pair_ids(0)
     theirs = own.at[pl.ds((1 - core) * rows, rows), :]
     remote(theirs, theirs, s_send.at[0], s_part.at[n_own], "pair").wait_recv()
     load_g.wait()
     load_u.wait()
     load_e.start()
+    turn([hits(0, c) for c in range(2)])
     for c in range(2):
-        mask[pl.ds(c * rows, rows), :] = turn(0, c)
+        spread(c, 0, rows, c * rows)
     hidden(own[...], 2 * rows, 0)
     gram(2 * rows, True)
 
@@ -329,17 +341,22 @@
 
     def take(role, step):
         filled, ids = arrivals(role, step)
-        for j, k in ids:
+        early = ids if step == 0 else []
+        for j, k in early:
             wait_ids(number(j, k))
         for slot in filled:
             wait_piece(*slot)
         for item in sends(role, step):
             for copy in send_copies(role, item):
                 copy.start()
-        for j, k in ids:
+        for j, k in early:
             pair_ids(number(j, k)).start()
         for slot in filled:
             pair_piece(*slot).start()
+        for j, k in ids:
+            if (j, k) not in early:
+                wait_ids(number(j, k))
+                pair_ids(number(j, k)).start()
 
     def join(role, step):
         filled, ids = arrivals(role, step)
@@ -363,15 +380,15 @@
                 def _():
                     act(role, step)
 
-    full = range(STEPS - 1)
+    full = range(STEPS - 2)
 
     def loop(s, carry):
         at_step(take, s, full)
         at_step(lambda role, step: drain(role, step - late), s, full[late - 1:])
 
-        @pl.when(jnp.logical_and(s > 0, s % 2 == 0))
+        @pl.when(s > 0)
         def _():
-            gram(2 * lot, False)
+            gram(lot, False, pl.multiple_of((s + 1) % 2 * lot, lot))
 
         @pl.when(s == 1)
         def _():
@@ -385,21 +402,43 @@
             lax.fori_loop(0, features // LANES, narrow, 0)
 
         at_step(join, s, full)
-        marks(s, half)
+
+        @pl.when(s == 0)
+        def _():
+            marks(0, half)
+
         hidden(tok[s], lot, pl.multiple_of((s % 2) * lot, lot))
+        marks(s + 1, half)
         return carry
 
-    lax.fori_loop(0, STEPS - 1, loop, 0)
+    lax.fori_loop(0, STEPS - 2, loop, 0)
     last = STEPS - 1
     part = 6 * quarter
-    for q in range(2):
-        when_role(take, last + q)
-        gram(part if q else lot, False, lot if q else 0)
-        when_role(drain, last + q - late)
-        when_role(join, last + q)
-        marks(last, quarter, q)
-        hidden(tok[last, pl.ds(q * part, part), :], part, lot if q == 0 else lot + part)
-    gram(part, False, lot + part)
+    def side(c, s, q, base, between=None):
+        count = lot // 2 if q is None else part // 2
+        skip = 0 if q is None else q * part
+        rows_at = pl.multiple_of(skip + c * count, count)
+        hidden(
+            tok[s, pl.ds(rows_at, count), :], count, pl.multiple_of(base + rows_at, count),
+            pl.multiple_of(base + rows_at, count), between,
+        )
+
+    when_role(take, last - 1)
+    side(core, last - 1, None, 0)
+    gram(lot, False, lot)
+    when_role(join, last - 1)
+    marks(last, quarter, 2, lot)
+    side(1 - core, last - 1, None, 0, lambda: when_role(take, last))
+    side(core, last, 0, lot)
+    gram(lot, False)
+    when_role(join, last)
+    side(1 - core, last, 0, lot, lambda: when_role(take, last + 1))
+    side(core, last, 1, lot)
+    for step in range(last - 1 - late, last + 1):
+        when_role(drain, step)
+    when_role(join, last + 1)
+    side(1 - core, last, 1, lot)
+    gram(lot, False, lot)
     count = jnp.sum((idb[...] == expert).astype(jnp.float32))
     for n in range(bands):
         for m in range(n, bands):
@@ -410,8 +449,7 @@
     for role, here in roles:
         @pl.when(here)
         def _():
-            for step in range(STEPS + 1 - late, STEPS + 1):
-                drain(role, step)
+            drain(role, last + 1)
 
 
 def finish_kernel(gram_ref, error_ref, out_hbm, done, sem):
@@ -456,8 +494,8 @@
             pltpu.VMEM((6 * rows, features), jnp.bfloat16),
             pltpu.VMEM((features, features), jnp.float32),
             pltpu.VMEM((features, width), jnp.float32),
-            pltpu.VMEM((6, rows, LANES), jnp.float32),
-            pltpu.VMEM((3 * rows, LANES), jnp.float32),
+            pltpu.VMEM((rows, 8), jnp.float32),
+            pltpu.VMEM((6 * rows, LANES), jnp.float32),
             dma((n_sends,)), dma((STEPS + 1, 3)), dma((16,)), dma((pieces,)), dma((pieces,)), dma((5,)),
         ],
         compiler_params=pltpu.CompilerParams(

time: 74.6 us -> 72.6 us (0.973)
  Pallas kernels: 73.9 us -> 72.3 us
    pallas_call x1, Pallas kernels: 70.2 us -> 68.5 us  [fused_local(): pl.pallas_call(gather_kernel, out_shape=(jax.ShapeDtypeStruct((features,...]
where the time goes in v3:
time: 72.6 us; the launch traced here: 72.4 us
  Pallas kernels  72.3 us (100%)
    pallas_call x1, Pallas kernels, fused_local(): pl.pallas_call(gather_kernel, out_shape=(jax.ShapeDtypeStruct((features,...  68.5 us
    pallas_call x1, Pallas kernels, fused_local(): pl.pallas_call(finish_kernel, out_shape=jax.ShapeDtypeStruct(down_error.s...  3.78 us

profile of v3, /device:TPU:0, one launch (start us, length us, event | category | flops | bytes accessed | tf_op | source)
XLA Modules:
  0.0 72.4 jit_solution(7849219406058327508)
XLA Ops:
  0.0 68.5 %shard_map.55 = (bf16[768,768]{1,0:T(8,128)(2,1)S(1)}, bf16[768,2048]{1,0:T(8,128)(2,1)S(1)}) custom-call(bf16[128,2048]{1,0:T(8,128)(2,1)} %x_hbm.1, s32[8,128]{1,0:T(8,128)} %bitcast.8, bf16[2048,768]{1,0:T(8,128)(2,1)} %bitcast.6, bf16[2048,768]{1,0:T(8,128)(2,1)} %bitcast.7, f32[768,2048]{1,0:T(8,128)} %bitcast.5), custom_call_target="tpu_custom_call" | custom-call | tf_op jit(solution)/shard_map/pallas_call | solution.py:480
  68.5 3.8 %shard_map.56 = f32[768,2048]{1,0:T(8,128)} custom-call(bf16[768,768]{1,0:T(8,128)(2,1)S(1)} %get-tuple-element.7.gram_ref, bf16[768,2048]{1,0:T(8,128)(2,1)S(1)} %get-tuple-element.8.error_ref), custom_call_target="tpu_custom_call" | custom-call | tf_op jit(solution)/shard_map/pallas_call | solution.py:508

commit v4 on v3

--- a/solution.py
+++ b/solution.py
@@ -126,7 +126,7 @@
 def gather_kernel(
     x_hbm, ids_hbm, wg_hbm, wu_hbm, e_hbm, out_ref, error_ref,
     own, tok, idb, wg, wu, hid, acc, error, turned, mask,
-    s_send, s_recv, s_idr, s_pair, s_part, s_load,
+    s_send, s_recv, s_idr, s_part, s_partid, s_load,
 ):
     gx = lax.axis_index("gx")
     z = lax.axis_index("gy")
@@ -172,22 +172,14 @@
     def number(j, k):
         return j * 4 + k
 
-    order = {}
-    for role in (CORNER, MIDDLE):
-        n = 0
-        for step in range(-1, STEPS):
-            for item in sends(role, step):
-                order[role, item] = n
-                n += 2
-
     def send_copies(role, item):
         queue, (j, k), h, there = item
         far = receiver(role, queue)
-        n = order[role, item]
         if h is None:
-            src = idb.at[number(j, k), core]
-            return [remote(src, idb.at[number(*there), core], s_send.at[n], s_idr.at[number(*there)], queue)]
+            src, dst = idb.at[number(j, k), core], idb.at[number(*there), core]
+            return [remote(src, dst, s_send.at[1], s_idr.at[ids_arrival(far, *there)], queue)]
         s, link = place(far, *there, h)
+        come = arrival(far, *there, h)
         mine = None if (j, k) == (0, 0) else place(role, j, k, h)
         copies = []
         for q in cuts(s, 0 if mine is None else mine[0]):
@@ -197,37 +189,34 @@
                 src = own.at[pl.ds(core * rows + h * half, half), :]
             else:
                 src = own.at[pl.ds(core * rows + h * half + q * quarter, quarter), :]
-            to = s + q if s == STEPS - 1 else s
-            copies.append(remote(src, spot(s, link, core, q), s_send.at[n + (q or 0)], s_recv.at[to, link], queue))
+            step = come + (q if come == STEPS - 1 else 0)
+            copies.append(remote(src, spot(s, link, core, q), s_send.at[0], s_recv.at[step], queue))
         return copies
 
-    def pair_piece(s, link, q):
-        n = (s + (q or 0)) * 3 + link
-        return remote(spot(s, link, core, q), spot(s, link, core, q), s_pair.at[n], s_part.at[n], "pair")
-
-    def pair_ids(b):
-        n = 3 * STEPS + 3 + b
-        return remote(idb.at[b, core], idb.at[b, core], s_pair.at[n], s_part.at[n], "pair")
-
-    n_own = 3 * STEPS + 19
+    def pair_piece(step, slot):
+        return remote(spot(*slot[:2], core, slot[2]), spot(*slot[:2], core, slot[2]), s_send.at[2], s_part.at[step], "pair")
+
+    def pair_ids(step, b):
+        return remote(idb.at[b, core], idb.at[b, core], s_send.at[3], s_partid.at[step], "pair")
+
     mine = own.at[pl.ds(core * rows, rows), :]
-    pair_own = remote(mine, mine, s_pair.at[n_own], s_part.at[n_own], "pair")
-
-    def wait_piece(s, link, q):
-        here = spot(s, link, core, q)
-        remote(here, here, s_send.at[0], s_recv.at[s + (q or 0), link], "pair").wait_recv()
-
-    def wait_ids(b):
-        remote(idb.at[b, core], idb.at[b, core], s_send.at[0], s_idr.at[b], "pair").wait_recv()
-
-    def wait_pair_piece(s, link, q):
-        n = (s + (q or 0)) * 3 + link
-        there = spot(s, link, 1 - core, q)
-        remote(there, there, s_send.at[0], s_part.at[n], "pair").wait_recv()
-
-    def wait_pair_ids(b):
-        n = 3 * STEPS + 3 + b
-        remote(idb.at[b, 1 - core], idb.at[b, 1 - core], s_send.at[0], s_part.at[n], "pair").wait_recv()
+    pair_own = remote(mine, mine, s_send.at[4], s_part.at[STEPS + 1], "pair")
+
+    def size_of(filled):
+        return sum(half if q is None else quarter for _, _, q in filled)
+
+    def counted(count):
+        views = [tok.at[pl.ds(0, count // lot)]] if count >= lot else []
+        return views + ([tok.at[0, pl.ds(0, count % lot), :]] if count % lot else [])
+
+    def wait_rows(sem, count):
+        for view in counted(count):
+            remote(view, view, s_send.at[0], sem, "pair").wait_recv()
+
+    def wait_ids(sem, count):
+        if count:
+            view = idb.at[pl.ds(0, count), 0]
+            remote(view, view, s_send.at[0], sem, "pair").wait_recv()
 
     bands = 3
     features = hid.shape[1]
@@ -243,7 +232,7 @@
     def spread(group, first, count, to):
         mask[pl.ds(to, count), :] = jnp.broadcast_to(turned[pl.ds(first, count), group:group + 1], (count, LANES))
 
-    def hidden(rows_in, count, base, first=0, between=None):
+    def hidden(rows_in, count, base, first=0, between=None, after=1):
         live = jnp.concatenate([mask[pl.ds(first, count), :]] * (band // LANES), axis=1)
         for n in range(bands):
             cols = pl.ds(n * band, band)
@@ -251,7 +240,7 @@
             upward = jnp.dot(rows_in, wu[:, cols], preferred_element_type=jnp.float32)
             value = gate / (1.0 + jnp.exp(-gate)) * upward
             hid[pl.ds(base, count), cols] = jnp.where(live > 0.5, value, 0.0).astype(jnp.bfloat16)
-            if between is not None and n == bands - 2:
+            if between is not None and n == after:
                 between()
 
     def gram(count, start, base=0):
@@ -298,8 +287,6 @@
     load_e = pltpu.make_async_copy(e_hbm, error, s_load.at[4])
     local.start()
     local_ids.start()
-    load_g.start()
-    load_u.start()
     local.wait()
     local_ids.wait()
     pl.semaphore_wait(barrier, 4 + inner)
@@ -311,11 +298,13 @@
             for item in sends(role, -1):
                 [copy.start() for copy in send_copies(role, item)]
 
-    pair_ids(0).start()
+    pair_ids(STEPS + 1, 0).start()
     pair_own.start()
-    wait_pair_ids(0)
+    load_g.start()
+    load_u.start()
+    wait_ids(s_partid.at[STEPS + 1], 1)
     theirs = own.at[pl.ds((1 - core) * rows, rows), :]
-    remote(theirs, theirs, s_send.at[0], s_part.at[n_own], "pair").wait_recv()
+    remote(theirs, theirs, s_send.at[4], s_part.at[STEPS + 1], "pair").wait_recv()
     load_g.wait()
     load_u.wait()
     load_e.start()
@@ -325,47 +314,41 @@
     hidden(own[...], 2 * rows, 0)
     gram(2 * rows, True)
 
-    def drain(role, step):
-        for item in sends(role, step):
-            for copy in send_copies(role, item):
-                copy.wait_send()
-        if step < 0:
-            pair_ids(0).wait_send()
-            pair_own.wait_send()
-            return
-        filled, ids = arrivals(role, step)
-        for j, k in ids:
-            pair_ids(number(j, k)).wait_send()
-        for slot in filled:
-            pair_piece(*slot).wait_send()
+    def drain(role):
+        items = [item for step in range(-1, STEPS) for item in sends(role, step)]
+        count = sum(half for item in items if item[2] is not None)
+        pairs = sum(size_of(arrivals(role, step)[0]) for step in range(STEPS + 1))
+        for n, total in ((0, count), (2, pairs)):
+            for view in counted(total):
+                remote(view, view, s_send.at[n], s_part.at[0], "pair").wait_send()
+        for n, total in ((1, sum(item[2] is None for item in items)), (3, 16)):
+            whole, rest = total // 2, total % 2
+            for view in [idb.at[pl.ds(0, whole)]] + [idb.at[0, 0]] * rest:
+                remote(view, view, s_send.at[n], s_part.at[0], "pair").wait_send()
+        pair_own.wait_send()
 
     def take(role, step):
         filled, ids = arrivals(role, step)
-        early = ids if step == 0 else []
-        for j, k in early:
-            wait_ids(number(j, k))
-        for slot in filled:
-            wait_piece(*slot)
+        if step == 0:
+            wait_ids(s_idr.at[step], len(ids))
+        wait_rows(s_recv.at[step], size_of(filled))
         for item in sends(role, step):
             for copy in send_copies(role, item):
                 copy.start()
-        for j, k in early:
-            pair_ids(number(j, k)).start()
+        if step == 0:
+            for j, k in ids:
+                pair_ids(step, number(j, k)).start()
         for slot in filled:
-            pair_piece(*slot).start()
-        for j, k in ids:
-            if (j, k) not in early:
-                wait_ids(number(j, k))
-                pair_ids(number(j, k)).start()
+            pair_piece(step, slot).start()
+        if step and ids:
+            wait_ids(s_idr.at[step], len(ids))
+            for j, k in ids:
+                pair_ids(step, number(j, k)).start()
 
     def join(role, step):
         filled, ids = arrivals(role, step)
-        for j, k in ids:
-            wait_pair_ids(number(j, k))
-        for slot in filled:
-            wait_pair_piece(*slot)
-
-    late = 5
+        wait_ids(s_partid.at[step], len(ids))
+        wait_rows(s_part.at[step], size_of(filled))
 
     def when_role(act, *args):
         for role, here in roles:
@@ -384,7 +367,6 @@
 
     def loop(s, carry):
         at_step(take, s, full)
-        at_step(lambda role, step: drain(role, step - late), s, full[late - 1:])
 
         @pl.when(s > 0)
         def _():
@@ -414,13 +396,13 @@
     lax.fori_loop(0, STEPS - 2, loop, 0)
     last = STEPS - 1
     part = 6 * quarter
-    def side(c, s, q, base, between=None):
+    def side(c, s, q, base, between=None, after=1):
         count = lot // 2 if q is None else part // 2
         skip = 0 if q is None else q * part
         rows_at = pl.multiple_of(skip + c * count, count)
         hidden(
             tok[s, pl.ds(rows_at, count), :], count, pl.multiple_of(base + rows_at, count),
-            pl.multiple_of(base + rows_at, count), between,
+            pl.multiple_of(base + rows_at, count), between, after,
         )
 
     when_role(take, last - 1)
@@ -428,14 +410,11 @@
     gram(lot, False, lot)
     when_role(join, last - 1)
     marks(last, quarter, 2, lot)
-    side(1 - core, last - 1, None, 0, lambda: when_role(take, last))
-    side(core, last, 0, lot)
+    side(1 - core, last - 1, None, 0, lambda: when_role(take, last), 0)
     gram(lot, False)
     when_role(join, last)
-    side(1 - core, last, 0, lot, lambda: when_role(take, last + 1))
+    hidden(tok[last, pl.ds(0, part), :], part, lot, lot, lambda: when_role(take, last + 1), 1)
     side(core, last, 1, lot)
-    for step in range(last - 1 - late, last + 1):
-        when_role(drain, step)
     when_role(join, last + 1)
     side(1 - core, last, 1, lot)
     gram(lot, False, lot)
@@ -446,26 +425,27 @@
             out_ref[pl.ds(n * band, band), pl.ds(m * band, band)] = part.astype(out_ref.dtype)
             if m > n:
                 out_ref[pl.ds(m * band, band), pl.ds(n * band, band)] = part.T.astype(out_ref.dtype)
-    for role, here in roles:
-        @pl.when(here)
-        def _():
-            drain(role, last + 1)
+    when_role(drain)
 
 
 def finish_kernel(gram_ref, error_ref, out_hbm, done, sem):
-    turns, _, cols = done.shape
-
-    def put(n):
-        return pltpu.make_async_copy(done.at[n], out_hbm.at[:, pl.ds(n * cols, cols)], sem.at[n])
-
-    for n in range(turns):
-        done[n] = jnp.dot(
-            gram_ref[...], error_ref[:, pl.ds(n * cols, cols)],
+    turns, features, cols = done.shape
+
+    def put(n, first, count, at):
+        return pltpu.make_async_copy(
+            done.at[n, pl.ds(first, count), :], out_hbm.at[pl.ds(first, count), pl.ds(n * cols, cols)], sem.at[at]
+        )
+
+    blocks = [(n, 0, features) for n in range(turns - 1)]
+    blocks += [(turns - 1, first, features // 2) for first in (0, features // 2)]
+    for at, (n, first, count) in enumerate(blocks):
+        done[n, pl.ds(first, count), :] = jnp.dot(
+            gram_ref[pl.ds(first, count), :], error_ref[:, pl.ds(n * cols, cols)],
             preferred_element_type=jnp.float32,
         )
-        put(n).start()
-    for n in range(turns):
-        put(n).wait()
+        put(n, first, count, at).start()
+    for at, block in enumerate(blocks):
+        put(*block, at).wait()
 
 
 def fused_local(tokens, expert_ids, w_gate, w_up, down_error):
@@ -475,8 +455,6 @@
     vmem = pl.BlockSpec(memory_space=pltpu.VMEM)
     hbm = pl.BlockSpec(memory_space=pltpu.HBM)
     dma = pltpu.SemaphoreType.DMA
-    n_sends = 2 * max(sum(len(sends(role, step)) for step in range(-1, STEPS)) for role in (CORNER, MIDDLE))
-    pieces = 3 * STEPS + 20
     mean_gram, narrow_error = pl.pallas_call(
         gather_kernel,
         out_shape=(
@@ -496,7 +474,7 @@
             pltpu.VMEM((features, width), jnp.float32),
             pltpu.VMEM((rows, 8), jnp.float32),
             pltpu.VMEM((6 * rows, LANES), jnp.float32),
-            dma((n_sends,)), dma((STEPS + 1, 3)), dma((16,)), dma((pieces,)), dma((pieces,)), dma((5,)),
+            dma((5,)), dma((STEPS + 1,)), dma((STEPS,)), dma((STEPS + 2,)), dma((STEPS + 2,)), dma((5,)),
         ],
         compiler_params=pltpu.CompilerParams(
             collective_id=0, has_side_effects=True, vmem_limit_bytes=VMEM_LIMIT
@@ -510,7 +488,7 @@
         out_shape=jax.ShapeDtypeStruct(down_error.shape[1:], jnp.float32),
         in_specs=[vmem, vmem],
         out_specs=hbm,
-        scratch_shapes=[pltpu.VMEM((down_error.shape[2] // FINISH_COLS, features, FINISH_COLS), jnp.float32), dma((down_error.shape[2] // FINISH_COLS,))],
+        scratch_shapes=[pltpu.VMEM((down_error.shape[2] // FINISH_COLS, features, FINISH_COLS), jnp.float32), dma((down_error.shape[2] // FINISH_COLS + 1,))],
         compiler_params=pltpu.CompilerParams(vmem_limit_bytes=FINISH_LIMIT),
     )(mean_gram, narrow_error)[None]
 

time: 72.6 us -> 70 us (0.964)
  Pallas kernels: 72.3 us -> 69.9 us
    pallas_call x1, Pallas kernels: 68.5 us -> 66.2 us  [fused_local(): pl.pallas_call(gather_kernel, out_shape=(jax.ShapeDtypeStruct((features,...]
where the time goes in v4:
time: 70 us; the launch traced here: 69.9 us
  Pallas kernels  69.9 us (100%)
    pallas_call x1, Pallas kernels, fused_local(): pl.pallas_call(gather_kernel, out_shape=(jax.ShapeDtypeStruct((features,...  66.2 us
    pallas_call x1, Pallas kernels, fused_local(): pl.pallas_call(finish_kernel, out_shape=jax.ShapeDtypeStruct(down_error.s...  3.68 us

profile of v4, /device:TPU:0, one launch (start us, length us, event | category | flops | bytes accessed | tf_op | source)
XLA Modules:
  0.0 69.9 jit_solution(3952346370111867803)
XLA Ops:
  0.0 66.2 %shard_map.55 = (bf16[768,768]{1,0:T(8,128)(2,1)S(1)}, bf16[768,2048]{1,0:T(8,128)(2,1)S(1)}) custom-call(bf16[128,2048]{1,0:T(8,128)(2,1)} %x_hbm.1, s32[8,128]{1,0:T(8,128)} %bitcast.8, bf16[2048,768]{1,0:T(8,128)(2,1)} %bitcast.6, bf16[2048,768]{1,0:T(8,128)(2,1)} %bitcast.7, f32[768,2048]{1,0:T(8,128)} %bitcast.5), custom_call_target="tpu_custom_call" | custom-call | tf_op jit(solution)/shard_map/pallas_call | solution.py:458
  66.2 3.7 %shard_map.56 = f32[768,2048]{1,0:T(8,128)} custom-call(bf16[768,768]{1,0:T(8,128)(2,1)S(1)} %get-tuple-element.7.gram_ref, bf16[768,2048]{1,0:T(8,128)(2,1)S(1)} %get-tuple-element.8.error_ref), custom_call_target="tpu_custom_call" | custom-call | tf_op jit(solution)/shard_map/pallas_call | solution.py:486

commit v5 on v4

--- a/solution.py
+++ b/solution.py
@@ -88,8 +88,8 @@
         if step == 2:
             put("in", (3, 0), (0, 1), (3, 1))
         if step == 7:
-            put("x", (2, 3), (0,), (3, 3))
-            put("y", (1, 3), (1,), (3, 3), ids=False)
+            put("x", (2, 3), (0,), (3, 3), ids=False)
+            put("y", (1, 3), (1,), (3, 3))
         return out
     if step in (0, 1):
         put("out", (0, 2), (step,), (0, 2), ids=step == 0)
@@ -194,13 +194,13 @@
         return copies
 
     def pair_piece(step, slot):
-        return remote(spot(*slot[:2], core, slot[2]), spot(*slot[:2], core, slot[2]), s_send.at[2], s_part.at[step], "pair")
+        return remote(spot(*slot[:2], core, slot[2]), spot(*slot[:2], core, slot[2]), s_send.at[2], s_part.at[step % 2], "pair")
 
     def pair_ids(step, b):
-        return remote(idb.at[b, core], idb.at[b, core], s_send.at[3], s_partid.at[step], "pair")
+        return remote(idb.at[b, core], idb.at[b, core], s_send.at[3], s_partid.at[step % 2], "pair")
 
     mine = own.at[pl.ds(core * rows, rows), :]
-    pair_own = remote(mine, mine, s_send.at[4], s_part.at[STEPS + 1], "pair")
+    pair_own = remote(mine, mine, s_send.at[4], s_part.at[1], "pair")
 
     def size_of(filled):
         return sum(half if q is None else quarter for _, _, q in filled)
@@ -281,10 +281,10 @@
         pl.semaphore_signal(barrier, inc=1, device_id=target["out"], device_id_type=MESH)
 
     local = pltpu.make_async_copy(x_hbm, mine, s_load.at[0])
-    local_ids = pltpu.make_async_copy(ids_hbm, idb.at[0, core], s_load.at[1])
-    load_g = pltpu.make_async_copy(wg_hbm, wg, s_load.at[2])
-    load_u = pltpu.make_async_copy(wu_hbm, wu, s_load.at[3])
-    load_e = pltpu.make_async_copy(e_hbm, error, s_load.at[4])
+    local_ids = pltpu.make_async_copy(ids_hbm, idb.at[0, core], s_load.at[0])
+    load_g = pltpu.make_async_copy(wg_hbm, wg, s_load.at[1])
+    load_u = pltpu.make_async_copy(wu_hbm, wu, s_load.at[1])
+    load_e = pltpu.make_async_copy(e_hbm, error, s_load.at[1])
     local.start()
     local_ids.start()
     local.wait()
@@ -298,13 +298,13 @@
             for item in sends(role, -1):
                 [copy.start() for copy in send_copies(role, item)]
 
-    pair_ids(STEPS + 1, 0).start()
+    pair_ids(1, 0).start()
     pair_own.start()
     load_g.start()
     load_u.start()
-    wait_ids(s_partid.at[STEPS + 1], 1)
+    wait_ids(s_partid.at[1], 1)
     theirs = own.at[pl.ds((1 - core) * rows, rows), :]
-    remote(theirs, theirs, s_send.at[4], s_part.at[STEPS + 1], "pair").wait_recv()
+    remote(theirs, theirs, s_send.at[4], s_part.at[1], "pair").wait_recv()
     load_g.wait()
     load_u.wait()
     load_e.start()
@@ -347,8 +347,8 @@
 
     def join(role, step):
         filled, ids = arrivals(role, step)
-        wait_ids(s_partid.at[step], len(ids))
-        wait_rows(s_part.at[step], size_of(filled))
+        wait_ids(s_partid.at[step % 2], len(ids))
+        wait_rows(s_part.at[step % 2], size_of(filled))
 
     def when_role(act, *args):
         for role, here in roles:
@@ -417,35 +417,39 @@
     side(core, last, 1, lot)
     when_role(join, last + 1)
     side(1 - core, last, 1, lot)
-    gram(lot, False, lot)
-    count = jnp.sum((idb[...] == expert).astype(jnp.float32))
+    share = 1.0 / jnp.sum((idb[...] == expert).astype(jnp.float32))
     for n in range(bands):
         for m in range(n, bands):
-            part = acc[pl.ds(n * band, band), pl.ds(m * band, band)] / count
-            out_ref[pl.ds(n * band, band), pl.ds(m * band, band)] = part.astype(out_ref.dtype)
+            down, across = pl.ds(n * band, band), pl.ds(m * band, band)
+            part = acc[down, across] + lax.dot_general(
+                hid[pl.ds(lot, lot), down], hid[pl.ds(lot, lot), across],
+                (((0,), (0,)), ((), ())), preferred_element_type=jnp.float32,
+            )
+            part = part * share
+            out_ref[down, across] = part.astype(out_ref.dtype)
             if m > n:
-                out_ref[pl.ds(m * band, band), pl.ds(n * band, band)] = part.T.astype(out_ref.dtype)
+                out_ref[across, down] = part.T.astype(out_ref.dtype)
     when_role(drain)
 
 
 def finish_kernel(gram_ref, error_ref, out_hbm, done, sem):
     turns, features, cols = done.shape
-
-    def put(n, first, count, at):
+    tall = features // 3
+    blocks = [(n, first) for first in range(0, features, tall) for n in range(turns)]
+
+    def put(at, n, first):
         return pltpu.make_async_copy(
-            done.at[n, pl.ds(first, count), :], out_hbm.at[pl.ds(first, count), pl.ds(n * cols, cols)], sem.at[at]
+            done.at[n, pl.ds(first, tall), :], out_hbm.at[pl.ds(first, tall), pl.ds(n * cols, cols)], sem.at[at]
         )
 
-    blocks = [(n, 0, features) for n in range(turns - 1)]
-    blocks += [(turns - 1, first, features // 2) for first in (0, features // 2)]
-    for at, (n, first, count) in enumerate(blocks):
-        done[n, pl.ds(first, count), :] = jnp.dot(
-            gram_ref[pl.ds(first, count), :], error_ref[:, pl.ds(n * cols, cols)],
+    for at, (n, first) in enumerate(blocks):
+        done[n, pl.ds(first, tall), :] = jnp.dot(
+            gram_ref[pl.ds(first, tall), :], error_ref[:, pl.ds(n * cols, cols)],
             preferred_element_type=jnp.float32,
         )
-        put(n, first, count, at).start()
+        put(at, n, first).start()
     for at, block in enumerate(blocks):
-        put(*block, at).wait()
+        put(at, *block).wait()
 
 
 def fused_local(tokens, expert_ids, w_gate, w_up, down_error):
@@ -474,7 +478,7 @@
             pltpu.VMEM((features, width), jnp.float32),
             pltpu.VMEM((rows, 8), jnp.float32),
             pltpu.VMEM((6 * rows, LANES), jnp.float32),
-            dma((5,)), dma((STEPS + 1,)), dma((STEPS,)), dma((STEPS + 2,)), dma((STEPS + 2,)), dma((5,)),
+            dma((5,)), dma((STEPS + 1,)), dma((STEPS,)), dma((2,)), dma((2,)), dma((2,)),
         ],
         compiler_params=pltpu.CompilerParams(
             collective_id=0, has_side_effects=True, vmem_limit_bytes=VMEM_LIMIT
@@ -488,7 +492,7 @@
         out_shape=jax.ShapeDtypeStruct(down_error.shape[1:], jnp.float32),
         in_specs=[vmem, vmem],
         out_specs=hbm,
-        scratch_shapes=[pltpu.VMEM((down_error.shape[2] // FINISH_COLS, features, FINISH_COLS), jnp.float32), dma((down_error.shape[2] // FINISH_COLS + 1,))],
+        scratch_shapes=[pltpu.VMEM((down_error.shape[2] // FINISH_COLS, features, FINISH_COLS), jnp.float32), dma((3 * (down_error.shape[2] // FINISH_COLS),))],
         compiler_params=pltpu.CompilerParams(vmem_limit_bytes=FINISH_LIMIT),
     )(mean_gram, narrow_error)[None]
 

time: 70 us -> 69.7 us (level)
  no operation moved by 1% of the time
where the time goes in v5:
time: 69.7 us; the launch traced here: 69.5 us
  Pallas kernels  69.5 us (100%)
    pallas_call x1, Pallas kernels, fused_local(): pl.pallas_call(gather_kernel, out_shape=(jax.ShapeDtypeStruct((features,...  66 us
    pallas_call x1, Pallas kernels, fused_local(): pl.pallas_call(finish_kernel, out_shape=jax.ShapeDtypeStruct(down_error.s...  3.51 us

profile of v5, /device:TPU:0, one launch (start us, length us, event | category | flops | bytes accessed | tf_op | source)
XLA Modules:
  0.0 69.5 jit_solution(13208983205314352030)
XLA Ops:
  0.0 66.0 %shard_map.55 = (bf16[768,768]{1,0:T(8,128)(2,1)S(1)}, bf16[768,2048]{1,0:T(8,128)(2,1)S(1)}) custom-call(bf16[128,2048]{1,0:T(8,128)(2,1)} %x_hbm.1, s32[8,128]{1,0:T(8,128)} %bitcast.8, bf16[2048,768]{1,0:T(8,128)(2,1)} %bitcast.6, bf16[2048,768]{1,0:T(8,128)(2,1)} %bitcast.7, f32[768,2048]{1,0:T(8,128)} %bitcast.5), custom_call_target="tpu_custom_call" | custom-call | tf_op jit(solution)/shard_map/pallas_call | solution.py:462
  66.0 3.5 %shard_map.56 = f32[768,2048]{1,0:T(8,128)} custom-call(bf16[768,768]{1,0:T(8,128)(2,1)S(1)} %get-tuple-element.7.gram_ref, bf16[768,2048]{1,0:T(8,128)(2,1)S(1)} %get-tuple-element.8.error_ref), custom_call_target="tpu_custom_call" | custom-call | tf_op jit(solution)/shard_map/pallas_call | solution.py:490

commit v6 on v5

--- a/solution.py
+++ b/solution.py
@@ -77,6 +77,8 @@
         put("in", (0, 0), (0, 1), (0, 1) if role == CORNER else (0, 2))
         if role == MIDDLE:
             put("out", (0, 0), (0, 1), (0, 1))
+        nth = {item: sum(other[0] == item[0] for other in out[:n]) for n, item in enumerate(out)}
+        out.sort(key=nth.get)
     if step == 0:
         put("x", (2, 0), (0,), (3, 0))
         put("y", (1, 0), (1,), (3, 0), ids=False)
@@ -437,19 +439,15 @@
     tall = features // 3
     blocks = [(n, first) for first in range(0, features, tall) for n in range(turns)]
 
-    def put(at, n, first):
-        return pltpu.make_async_copy(
-            done.at[n, pl.ds(first, tall), :], out_hbm.at[pl.ds(first, tall), pl.ds(n * cols, cols)], sem.at[at]
-        )
-
-    for at, (n, first) in enumerate(blocks):
+    for n, first in blocks:
         done[n, pl.ds(first, tall), :] = jnp.dot(
             gram_ref[pl.ds(first, tall), :], error_ref[:, pl.ds(n * cols, cols)],
             preferred_element_type=jnp.float32,
         )
-        put(at, n, first).start()
-    for at, block in enumerate(blocks):
-        put(at, *block).wait()
+        pltpu.make_async_copy(
+            done.at[n, pl.ds(first, tall), :], out_hbm.at[pl.ds(first, tall), pl.ds(n * cols, cols)], sem.at[0]
+        ).start()
+    pltpu.make_async_copy(done, done, sem.at[0]).wait()
 
 
 def fused_local(tokens, expert_ids, w_gate, w_up, down_error):
@@ -492,7 +490,7 @@
         out_shape=jax.ShapeDtypeStruct(down_error.shape[1:], jnp.float32),
         in_specs=[vmem, vmem],
         out_specs=hbm,
-        scratch_shapes=[pltpu.VMEM((down_error.shape[2] // FINISH_COLS, features, FINISH_COLS), jnp.float32), dma((3 * (down_error.shape[2] // FINISH_COLS),))],
+        scratch_shapes=[pltpu.VMEM((down_error.shape[2] // FINISH_COLS, features, FINISH_COLS), jnp.float32), dma((1,))],
         compiler_params=pltpu.CompilerParams(vmem_limit_bytes=FINISH_LIMIT),
     )(mean_gram, narrow_error)[None]
 

time: 69.7 us -> 69.6 us (level)
  no operation moved by 1% of the time
where the time goes in v6:
time: 69.6 us; the launch traced here: 69.4 us
  Pallas kernels  69.4 us (100%)
    pallas_call x1, Pallas kernels, fused_local(): pl.pallas_call(gather_kernel, out_shape=(jax.ShapeDtypeStruct((features,...  66 us
    pallas_call x1, Pallas kernels, fused_local(): pl.pallas_call(finish_kernel, out_shape=jax.ShapeDtypeStruct(down_error.s...  3.42 us

profile of v6, /device:TPU:0, one launch (start us, length us, event | category | flops | bytes accessed | tf_op | source)
XLA Modules:
  0.0 69.4 jit_solution(3501547867295314356)
XLA Ops:
  0.0 66.0 %shard_map.55 = (bf16[768,768]{1,0:T(8,128)(2,1)S(1)}, bf16[768,2048]{1,0:T(8,128)(2,1)S(1)}) custom-call(bf16[128,2048]{1,0:T(8,128)(2,1)} %x_hbm.1, s32[8,128]{1,0:T(8,128)} %bitcast.8, bf16[2048,768]{1,0:T(8,128)(2,1)} %bitcast.6, bf16[2048,768]{1,0:T(8,128)(2,1)} %bitcast.7, f32[768,2048]{1,0:T(8,128)} %bitcast.5), custom_call_target="tpu_custom_call" | custom-call | tf_op jit(solution)/shard_map/pallas_call | solution.py:460
  66.0 3.4 %shard_map.56 = f32[768,2048]{1,0:T(8,128)} custom-call(bf16[768,768]{1,0:T(8,128)(2,1)S(1)} %get-tuple-element.7.gram_ref, bf16[768,2048]{1,0:T(8,128)(2,1)S(1)} %get-tuple-element.8.error_ref), custom_call_target="tpu_custom_call" | custom-call | tf_op jit(solution)/shard_map/pallas_call | solution.py:488

commit v7 on v6

--- a/solution.py
+++ b/solution.py
@@ -413,12 +413,11 @@
     when_role(join, last - 1)
     marks(last, quarter, 2, lot)
     side(1 - core, last - 1, None, 0, lambda: when_role(take, last), 0)
-    gram(lot, False)
     when_role(join, last)
     hidden(tok[last, pl.ds(0, part), :], part, lot, lot, lambda: when_role(take, last + 1), 1)
-    side(core, last, 1, lot)
+    gram(lot, False)
     when_role(join, last + 1)
-    side(1 - core, last, 1, lot)
+    hidden(tok[last, pl.ds(part, part), :], part, lot + part, lot + part)
     share = 1.0 / jnp.sum((idb[...] == expert).astype(jnp.float32))
     for n in range(bands):
         for m in range(n, bands):

time: 69.6 us -> 69.7 us (level)
  no operation moved by 1% of the time
where the time goes in v7:
time: 69.7 us; the launch traced here: 69.5 us
  Pallas kernels  69.5 us (100%)
    pallas_call x1, Pallas kernels, fused_local(): pl.pallas_call(gather_kernel, out_shape=(jax.ShapeDtypeStruct((features,...  66.1 us
    pallas_call x1, Pallas kernels, fused_local(): pl.pallas_call(finish_kernel, out_shape=jax.ShapeDtypeStruct(down_error.s...  3.42 us

profile of v7, /device:TPU:0, one launch (start us, length us, event | category | flops | bytes accessed | tf_op | source)
XLA Modules:
  0.0 69.5 jit_solution(16403823594873587535)
XLA Ops:
  0.0 66.1 %shard_map.55 = (bf16[768,768]{1,0:T(8,128)(2,1)S(1)}, bf16[768,2048]{1,0:T(8,128)(2,1)S(1)}) custom-call(bf16[128,2048]{1,0:T(8,128)(2,1)} %x_hbm.1, s32[8,128]{1,0:T(8,128)} %bitcast.8, bf16[2048,768]{1,0:T(8,128)(2,1)} %bitcast.6, bf16[2048,768]{1,0:T(8,128)(2,1)} %bitcast.7, f32[768,2048]{1,0:T(8,128)} %bitcast.5), custom_call_target="tpu_custom_call" | custom-call | tf_op jit(solution)/shard_map/pallas_call | solution.py:459
  66.1 3.4 %shard_map.56 = f32[768,2048]{1,0:T(8,128)} custom-call(bf16[768,768]{1,0:T(8,128)(2,1)S(1)} %get-tuple-element.7.gram_ref, bf16[768,2048]{1,0:T(8,128)(2,1)S(1)} %get-tuple-element.8.error_ref), custom_call_target="tpu_custom_call" | custom-call | tf_op jit(solution)/shard_map/pallas_call | solution.py:487
